TPU v7x, 32 devices: a whole 2x2x4 slice. The times are simulated.
32 devices in a mesh: strike: 8 (over y, x, core), dip: 4 (over z).
Axes of the slice: x: 2, y: 2, z: 4, core: 2. Of those that a mesh axis runs over, the one named last changes fastest.
Arguments:
- velocity: float32 [12, 128, 1024], P(None, 'strike', 'dip'), may hold values from -6 to 6
- stress: float32 [3, 12, 128, 1024], P(None, None, 'strike', 'dip'), may hold values from -6 to 6
- shear_modulus: float32 [12, 128, 1024], P(None, 'strike', 'dip'), may hold values from 0.5 to 2
- buoyancy: float32 [12, 128, 1024], P(None, 'strike', 'dip'), may hold values from 0.5 to 2
- prestress: float32 [128, 1024], P('strike', 'dip'), may hold values from -6 to 6
- normal_stress: float32 [128, 1024], P('strike', 'dip'), may hold values from 0.5 to 2
- crit_slip: float32 [128, 1024], P('strike', 'dip'), may hold values from 0.25 to 4
- slip: float32 [128, 1024], P('strike', 'dip'), may hold values from 0 to 2
- traction: float32 [128, 1024], P('strike', 'dip'), may hold values from -6 to 6
- functional: float32 [128, 1024], P('strike', 'dip'), may hold values from -6 to 6
- flags: int32 [128, 1024], P('strike', 'dip'), may hold values 0 or 1
- history: float32 [64, 2, 1024, 128], P(None, None, ('strike', 'dip')), may hold values from -6 to 6
- kernel: bfloat16 [65, 1024, 128], P(None, ('strike', 'dip')), may hold values from -0.75 to 0.75
Outputs:
- new_velocity: float32 [12, 128, 1024], P(None, 'strike', 'dip')
- new_stress: float32 [3, 12, 128, 1024], P(None, None, 'strike', 'dip')
- new_slip: float32 [128, 1024], P('strike', 'dip')
- new_traction: float32 [128, 1024], P('strike', 'dip')
- new_functional: float32 [128, 1024], P('strike', 'dip')
Inputs may be any that keep to these rules, and one draw needn't show every extreme that they name: `flags`: 1 marks a fault cell on the slip-weakening branch, 0 a stuck cell.
All inputs are finite; a program needn't handle non-finite values. No bound on the sum of `flags` on one device may be relied on, other than what follows from the above.
Results may differ from a plain program's by a relative error of at most 0.0003.
Values sent between devices are 32-bit elements; how exact they have to be, the bound alone decides.
A program may use at most 64 MiB of HBM per device.

v0:
```python
import math

import jax
import jax.numpy as jnp
from jax import lax
from jax.sharding import PartitionSpec as P

STEPS = 2


coef_near = 2.0 / 3.0
coef_far = -1.0 / 12.0
courant = 0.3
static_friction = 0.677
dynamic_friction = 0.525
damping = 0.5
time_step = 0.3


def padded_2(block, sides, width):
    for axis, dim in sides:
        count = lax.axis_size(axis)
        forward = [(i, i + 1) for i in range(count - 1)]
        forward.append((count - 1, 0))
        backward = [(target, source) for source, target in forward]
        low = lax.ppermute(
            lax.slice_in_dim(block, block.shape[dim] - width, None, axis=dim), axis, forward
        )
        high = lax.ppermute(lax.slice_in_dim(block, 0, width, axis=dim), axis, backward)
        block = jnp.concatenate([low, block, high], axis=dim)
    return block


def central(padded, axis, start, count):

    def window(offset):
        return lax.slice_in_dim(padded, start + offset, start + offset + count, axis=axis)

    return coef_near * (window(1) - window(-1)) + coef_far * (window(2) - window(-2))


def normal_diff(field, ghost):
    zeros = jnp.zeros_like(ghost)
    padded = jnp.concatenate([ghost, ghost, field, zeros, zeros], axis=0)
    return central(padded, 0, 2, field.shape[0])


def fault_update(prestress, normal_stress, crit_slip, flags, slip, stress_z, functional):
    trial = prestress + stress_z[0] + functional
    weaken = jnp.maximum(0.0, 1.0 - jnp.abs(slip) / crit_slip)
    strength = normal_stress * (dynamic_friction + (static_friction - dynamic_friction) * weaken)
    clipped = jnp.clip(trial, -strength, strength)
    traction = jnp.where(flags == 1, clipped, trial)
    rate = (trial - traction) / damping
    return (traction, slip + time_step * rate)


def factor_pair(length):
    first = 1
    candidate = 1
    while candidate * candidate <= length:
        if length % candidate == 0:
            first = candidate
        candidate += 1
    return (first, length // first)


def phase_table(count_a, count_b, length, sign):
    product = lax.iota(jnp.int32, count_a)[:, None] * lax.iota(jnp.int32, count_b)[None, :] % length
    angles = sign * 2.0 * math.pi / length * product.astype(jnp.float32)
    return (jnp.cos(angles), jnp.sin(angles))


def contract(form, left, right):
    return jnp.einsum(form, left, right, precision=lax.Precision.HIGHEST)


def transform_last(real_part, imag_part, sign):
    length = real_part.shape[-1]
    outer, inner = factor_pair(length)
    leading = real_part.shape[:-1]
    real_part = real_part.reshape(leading + (outer, inner))
    imag_part = imag_part.reshape(leading + (outer, inner))
    first_cos, first_sin = phase_table(outer, outer, outer, sign)
    middle_real = contract("kt,...tq->...kq", first_cos, real_part) - contract(
        "kt,...tq->...kq", first_sin, imag_part
    )
    middle_imag = contract("kt,...tq->...kq", first_cos, imag_part) + contract(
        "kt,...tq->...kq", first_sin, real_part
    )
    twist_cos, twist_sin = phase_table(outer, inner, length, sign)
    middle_real, middle_imag = (
        middle_real * twist_cos - middle_imag * twist_sin,
        middle_real * twist_sin + middle_imag * twist_cos,
    )
    second_cos, second_sin = phase_table(inner, inner, inner, sign)
    out_real = contract("...kt,tm->...km", middle_real, second_cos) - contract(
        "...kt,tm->...km", middle_imag, second_sin
    )
    out_imag = contract("...kt,tm->...km", middle_real, second_sin) + contract(
        "...kt,tm->...km", middle_imag, second_cos
    )
    scale = 1.0 / math.sqrt(length)
    out_real = jnp.swapaxes(out_real, -1, -2).reshape(leading + (length,)) * scale
    out_imag = jnp.swapaxes(out_imag, -1, -2).reshape(leading + (length,)) * scale
    return (out_real, out_imag)


def body(
    velocity,
    stress,
    shear_modulus,
    buoyancy,
    prestress,
    normal_stress,
    crit_slip,
    slip,
    traction,
    functional,
    flags,
    history,
    kernel,
):
    strike_count = lax.axis_size("strike")
    dip_count = lax.axis_size("dip")
    depth, rows_x, cols_y = velocity.shape
    ky_local = history.shape[2]
    total_x = history.shape[3]
    total_y = cols_y * dip_count
    line_rows = rows_x // dip_count
    stress_x, stress_y, stress_z = (stress[0], stress[1], stress[2])
    ghost_zero = jnp.zeros((1, rows_x, cols_y), jnp.float32)
    spectra = []
    for iteration in range(STEPS):
        padded_x = padded_2(stress_x, (("strike", 1),), 2)
        padded_y = padded_2(stress_y, (("dip", 2),), 2)
        divergence = (
            central(padded_x, 1, 2, rows_x)
            + central(padded_y, 2, 2, cols_y)
            + normal_diff(stress_z, traction[None])
        )
        velocity = velocity + courant * buoyancy * divergence
        padded_v = padded_2(velocity, (("strike", 1), ("dip", 2)), 2)
        grad_x = central(padded_v[:, :, 2 : cols_y + 2], 1, 2, rows_x)
        grad_y = central(padded_v[:, 2 : rows_x + 2, :], 2, 2, cols_y)
        stress_x = stress_x + courant * shear_modulus * grad_x
        stress_y = stress_y + courant * shear_modulus * grad_y
        stress_z = stress_z + courant * shear_modulus * normal_diff(velocity, ghost_zero)
        traction, slip = fault_update(
            prestress, normal_stress, crit_slip, flags, slip, stress_z, functional
        )
        lines = lax.all_to_all(slip, "dip", split_axis=0, concat_axis=1, tiled=True)
        part_real, part_imag = transform_last(lines, jnp.zeros_like(lines), -1.0)
        stacked = jnp.stack([part_real, part_imag]).reshape(
            2, line_rows, strike_count, dip_count, ky_local
        )
        stacked = stacked.transpose(0, 2, 3, 4, 1).reshape(
            2, strike_count, dip_count, ky_local, 1, 1, line_rows
        )
        halfway = lax.all_to_all(stacked, "strike", split_axis=1, concat_axis=4, tiled=True)
        owned = lax.all_to_all(halfway, "dip", split_axis=2, concat_axis=5, tiled=True)
        owned = owned.reshape(2, ky_local, total_x)
        spec_real, spec_imag = transform_last(owned[0], owned[1], -1.0)
        spectra = [(spec_real, spec_imag)] + spectra
        weights = kernel[iteration + 1 :].astype(jnp.float32)
        stored = jnp.sum(weights[:, None] * history[: history.shape[0] - iteration], axis=0)
        sum_real = stored[0]
        sum_imag = stored[1]
        for offset, item in enumerate(spectra):
            weight = kernel[offset].astype(jnp.float32)
            sum_real = sum_real + weight * item[0]
            sum_imag = sum_imag + weight * item[1]
        back_real, back_imag = transform_last(sum_real, sum_imag, 1.0)
        leaving = jnp.stack([back_real, back_imag]).reshape(
            2, 1, 1, ky_local, strike_count, dip_count, line_rows
        )
        partway = lax.all_to_all(leaving, "strike", split_axis=4, concat_axis=1, tiled=True)
        returned = lax.all_to_all(partway, "dip", split_axis=5, concat_axis=2, tiled=True)
        returned = returned.reshape(2, total_y, line_rows).transpose(0, 2, 1)
        field_real, field_imag = transform_last(returned[0], returned[1], 1.0)
        functional = lax.all_to_all(field_real, "dip", split_axis=1, concat_axis=0, tiled=True)
    return (velocity, jnp.stack([stress_x, stress_y, stress_z]), slip, traction, functional)


def solution(mesh):
    return jax.shard_map(
        body,
        mesh=mesh,
        in_specs=(
            P(None, "strike", "dip"),
            P(None, None, "strike", "dip"),
            P(None, "strike", "dip"),
            P(None, "strike", "dip"),
            P("strike", "dip"),
            P("strike", "dip"),
            P("strike", "dip"),
            P("strike", "dip"),
            P("strike", "dip"),
            P("strike", "dip"),
            P("strike", "dip"),
            P(None, None, ("strike", "dip"), None),
            P(None, ("strike", "dip"), None),
        ),
        out_specs=(
            P(None, "strike", "dip"),
            P(None, None, "strike", "dip"),
            P("strike", "dip"),
            P("strike", "dip"),
            P("strike", "dip"),
        ),
        check_vma=False,
    )
```

profile of v0, /device:TPU:0, one launch (start us, length us, event | category | flops | bytes accessed | tf_op | source)
XLA Modules:
  0.0 227.5 jit_solution(3571912595445253097)
XLA Ops:
  2.0 5.1 %collective-permute-start.2 = (f32[12,16,2]{2,1,0:T(8,128)S(1)}, f32[12,16,2]{2,1,0:T(8,128)S(1)}, u32[]{:S(2)}, u32[]{:S(2)}) collective-permute-start(f32[12,16,2]{2,1,0:T(8,128)S(1)} %get-tuple-element.33), channel_id=1, source_target_pairs={{1,0},{2,1},{3,2},{0,3},{5,4},{6,5},{7,6},{4,7},{9,8},{10,9},{11,1... | collective-permute-start | bytes 4616 | tf_op jit(solution)/shard_map/ppermute | solution.py:29
  7.1 1.7 collective-permute-start
  17.1 2.6 %collective-permute-start.4 = (f32[12,2,256]{2,1,0:T(2,128)}, f32[12,2,256]{2,1,0:T(2,128)}, u32[]{:S(2)}, u32[]{:S(2)}) collective-permute-start(f32[12,2,256]{2,1,0:T(2,128)} %get-tuple-element.30), channel_id=1, source_target_pairs={{4,0},{8,4},{12,8},{16,12},{20,16},{24,20},{28,24},{0,28},{5,1},{9... | collective-permute-start | bytes 73736 | tf_op jit(solution)/shard_map/ppermute | solution.py:29
  21.3 1.4 copy.324
  22.7 1.4 copy.214
  24.2 1.4 copy.233
  25.6 1.4 copy.251
  27.0 1.4 copy.254
  28.4 2.0 fusion.100
  31.1 1.4 multiply_add_fusion.7
  33.8 4.8 %all-to-all-start = ((f32[4,4,256]{2,1,0:T(4,128)}), f32[4,4,256]{2,1,0:T(4,128)}, u32[]{:S(2)}, u32[]{:S(2)}) async-start(f32[4,4,256]{2,1,0:T(4,128)} %all_to_all.144), calls=%async_computation | async-start | bytes 32768 | tf_op jit(solution)/shard_map/all_to_all | solution.py:152
  40.2 3.8 %collective-permute-start.8 = (f32[12,20,2]{2,1,0:T(8,128)}, f32[12,20,2]{2,1,0:T(8,128)}, u32[]{:S(2)}, u32[]{:S(2)}) collective-permute-start(f32[12,20,2]{2,1,0:T(8,128)} %get-tuple-element.21), channel_id=1, source_target_pairs={{1,0},{2,1},{3,2},{0,3},{5,4},{6,5},{7,6},{4,7},{9,8},{10,9},{11,1... | collective-permute-start | bytes 5768 | tf_op jit(solution)/shard_map/ppermute | solution.py:29
  44.0 1.6 fusion.606
  45.6 1.8 collective-permute-start.6
  48.8 1.4 reshape.340
  54.8 1.5 copy.223
  56.3 1.8 fusion.39
  58.1 1.5 copy.226
  59.7 1.6 copy_bitcast_fusion.7
  61.2 1.7 reshape.360
  62.9 3.9 %all-to-all-start.1 = ((f32[8,1,1024]{2,1,0:T(1,128)}), f32[8,1,1024]{2,1,0:T(1,128)}, u32[]{:S(2)}, u32[]{:S(2)}) async-start(f32[8,1,1024]{2,1,0:T(1,128)} %reshape.360), calls=%async_computation.1 | async-start | bytes 65536 | tf_op jit(solution)/shard_map/all_to_all | solution.py:160
  66.9 2.4 %fusion.128 = f32[12,16,256]{2,1,0:T(8,128)} fusion(f32[12,20,2]{2,1,0:T(8,128)} %collective-permute-done.9, f32[12,2,256]{2,1,0:T(2,128)} %collective-permute-done.4, f32[12,16,256]{2,1,0:T(8,128)S(1)} %fusion.49, f32[12,2,256]{2,1,0:T(2,128)} %collective-permute-done.5, f32[12,20,2]{2,1,0:T(8,128)} %collective-permute-done.8, ...), kind=kLoop, calls=%fused_computation.217 | loop fusion | flops 983040 | bytes 839424 | tf_op jit(solution)/shard_map/add | solution.py:147
  69.3 2.5 %all-to-all-done.1 = f32[8,1,1024]{2,1,0:T(1,128)} async-done(((f32[8,1,1024]{2,1,0:T(1,128)}), f32[8,1,1024]{2,1,0:T(1,128)}, u32[]{:S(2)}, u32[]{:S(2)}) %all-to-all-start.1) | async-done | bytes 32800 | tf_op jit(solution)/shard_map/all_to_all | solution.py:160
  72.3 1.5 reduce
  74.8 4.8 %all-to-all-start.2 = ((f32[4,1,2048]{2,1,0:T(1,128)}), f32[4,1,2048]{2,1,0:T(1,128)S(1)}, u32[]{:S(2)}, u32[]{:S(2)}) async-start(f32[4,1,2048]{2,1,0:T(1,128)} %reshape.362), calls=%async_computation.2 | async-start | bytes 65536 | tf_op jit(solution)/shard_map/all_to_all | solution.py:161
  79.6 1.7 fusion.607
  81.3 3.8 %collective-permute-start.10 = (f32[12,16,2]{2,1,0:T(8,128)}, f32[12,16,2]{2,1,0:T(8,128)}, u32[]{:S(2)}, u32[]{:S(2)}) collective-permute-start(f32[12,16,2]{2,1,0:T(8,128)} %get-tuple-element.27), channel_id=1, source_target_pairs={{1,0},{2,1},{3,2},{0,3},{5,4},{6,5},{7,6},{4,7},{9,8},{10,9},{11,1... | collective-permute-start | bytes 4616 | tf_op jit(solution)/shard_map/ppermute | solution.py:29
  92.1 3.9 %all-to-all-start.3 = ((f32[8,1,1024]{2,1,0:T(1,128)}), f32[8,1,1024]{2,1,0:T(1,128)}, u32[]{:S(2)}, u32[]{:S(2)}) async-start(f32[8,1,1024]{2,1,0:T(1,128)} %reshape.364), calls=%async_computation.3 | async-start | bytes 65536 | tf_op jit(solution)/shard_map/all_to_all | solution.py:177
  96.1 2.6 %fusion.64 = f32[12,16,256]{2,1,0:T(8,128)S(1)} fusion(f32[12,16,256]{2,1,0:T(8,128)S(1)} %fusion.49, f32[12,16,256]{2,1,0:T(8,128)} %copy-done.6, f32[1,16,256]{2,1,0:T(8,128)} %bitcast.422, f32[12,16,2]{2,1,0:T(8,128)} %collective-permute-done.11, f32[12,16,256]{2,1,0:T(8,128)} %fusion.128, f32[12,16,2]{2,1,0:T(8,128)} %collective-permute-done.10, ...), kind=kLoop, calls=%fused_computation.141 | loop fusion | flops 1523712 | bytes 1248256 | tf_op jit(solution)/shard_map/add | solution.py:142
  98.8 2.2 all-to-all-done.3
  100.9 2.1 reduce.2
  103.1 1.5 reshape.365
  104.6 1.6 copy_bitcast_fusion.4
  106.2 1.7 reshape.366
  107.8 4.8 %all-to-all-start.4 = ((f32[4,1,2048]{2,1,0:T(1,128)}), f32[4,1,2048]{2,1,0:T(1,128)}, u32[]{:S(2)}, u32[]{:S(2)}) async-start(f32[4,1,2048]{2,1,0:T(1,128)} %reshape.366), calls=%async_computation.4 | async-start | bytes 65536 | tf_op jit(solution)/shard_map/all_to_all | solution.py:178
  113.8 4.6 %all-to-all-done.4 = f32[4,1,2048]{2,1,0:T(1,128)} async-done(((f32[4,1,2048]{2,1,0:T(1,128)}), f32[4,1,2048]{2,1,0:T(1,128)}, u32[]{:S(2)}, u32[]{:S(2)}) %all-to-all-start.4) | async-done | bytes 32800 | tf_op jit(solution)/shard_map/all_to_all | solution.py:178
  118.4 2.1 reduce.3
  120.6 1.5 reshape.367
  123.8 1.7 reshape.342
  125.4 1.3 fusion.615
  126.8 1.4 reshape_squeeze.26
  128.2 1.8 fusion.226
  130.0 1.4 reshape_squeeze.27
  135.9 1.7 fusion.23
  137.6 1.5 copy.257
  139.1 1.5 mul.1696
  142.0 3.9 %all-to-all-start.5 = ((f32[4,4,256]{2,0,1:T(4,128)}), f32[4,4,256]{2,0,1:T(4,128)}, u32[]{:S(2)}, u32[]{:S(2)}) async-start(f32[4,4,256]{2,0,1:T(4,128)} %copy.258), calls=%async_computation.5 | async-start | bytes 32768 | tf_op jit(solution)/shard_map/all_to_all | solution.py:181
  145.9 2.0 fusion.82
  147.9 3.6 %all-to-all-done.5 = f32[4,4,256]{2,0,1:T(4,128)} async-done(((f32[4,4,256]{2,0,1:T(4,128)}), f32[4,4,256]{2,0,1:T(4,128)}, u32[]{:S(2)}, u32[]{:S(2)}) %all-to-all-start.5) | async-done | bytes 16416 | tf_op jit(solution)/shard_map/all_to_all | solution.py:181
  152.8 1.4 multiply_add_fusion.6
  155.6 3.8 %all-to-all-start.6 = ((f32[4,4,256]{2,1,0:T(4,128)}), f32[4,4,256]{2,1,0:T(4,128)}, u32[]{:S(2)}, u32[]{:S(2)}) async-start(f32[4,4,256]{2,1,0:T(4,128)} %all_to_all.164), calls=%async_computation.6 | async-start | bytes 32768 | tf_op jit(solution)/shard_map/all_to_all | solution.py:152
  160.5 4.6 %all-to-all-done.6 = f32[4,4,256]{2,1,0:T(4,128)} async-done(((f32[4,4,256]{2,1,0:T(4,128)}), f32[4,4,256]{2,1,0:T(4,128)}, u32[]{:S(2)}, u32[]{:S(2)}) %all-to-all-start.6) | async-done | bytes 16416 | tf_op jit(solution)/shard_map/all_to_all | solution.py:152
  170.5 3.3 %all-to-all-start.7 = ((f32[8,1,1024]{2,1,0:T(1,128)}), f32[8,1,1024]{2,1,0:T(1,128)S(1)}, u32[]{:S(2)}, u32[]{:S(2)}) async-start(f32[8,1,1024]{2,1,0:T(1,128)} %reshape.368), calls=%async_computation.7 | async-start | bytes 65536 | tf_op jit(solution)/shard_map/all_to_all | solution.py:160
  174.2 4.4 %all-to-all-done.7 = f32[8,1,1024]{2,1,0:T(1,128)S(1)} async-done(((f32[8,1,1024]{2,1,0:T(1,128)}), f32[8,1,1024]{2,1,0:T(1,128)S(1)}, u32[]{:S(2)}, u32[]{:S(2)}) %all-to-all-start.7) | async-done | bytes 32800 | tf_op jit(solution)/shard_map/all_to_all | solution.py:160
  180.3 3.4 %all-to-all-start.8 = ((f32[4,1,2048]{2,1,0:T(1,128)}), f32[4,1,2048]{2,1,0:T(1,128)S(1)}, u32[]{:S(2)}, u32[]{:S(2)}) async-start(f32[4,1,2048]{2,1,0:T(1,128)} %reshape.370), calls=%async_computation.8 | async-start | bytes 65536 | tf_op jit(solution)/shard_map/all_to_all | solution.py:161
  184.5 4.8 %all-to-all-done.8 = f32[4,1,2048]{2,1,0:T(1,128)S(1)} async-done(((f32[4,1,2048]{2,1,0:T(1,128)}), f32[4,1,2048]{2,1,0:T(1,128)S(1)}, u32[]{:S(2)}, u32[]{:S(2)}) %all-to-all-start.8) | async-done | bytes 32800 | tf_op jit(solution)/shard_map/all_to_all | solution.py:161
  195.3 3.3 %all-to-all-start.9 = ((f32[8,1,1024]{2,1,0:T(1,128)}), f32[8,1,1024]{2,1,0:T(1,128)S(1)}, u32[]{:S(2)}, u32[]{:S(2)}) async-start(f32[8,1,1024]{2,1,0:T(1,128)} %reshape.372), calls=%async_computation.9 | async-start | bytes 65536 | tf_op jit(solution)/shard_map/all_to_all | solution.py:177
  199.5 1.4 collective-permute-start.15
  200.9 2.6 %all-to-all-done.9 = f32[8,1,1024]{2,1,0:T(1,128)S(1)} async-done(((f32[8,1,1024]{2,1,0:T(1,128)}), f32[8,1,1024]{2,1,0:T(1,128)S(1)}, u32[]{:S(2)}, u32[]{:S(2)}) %all-to-all-start.9) | async-done | bytes 32800 | tf_op jit(solution)/shard_map/all_to_all | solution.py:177
  205.2 3.3 %all-to-all-start.10 = ((f32[4,1,2048]{2,1,0:T(1,128)}), f32[4,1,2048]{2,1,0:T(1,128)S(1)}, u32[]{:S(2)}, u32[]{:S(2)}) async-start(f32[4,1,2048]{2,1,0:T(1,128)} %reshape.374), calls=%async_computation.10 | async-start | bytes 65536 | tf_op jit(solution)/shard_map/all_to_all | solution.py:178
  208.5 1.4 fusion.118
  209.9 4.2 %all-to-all-done.10 = f32[4,1,2048]{2,1,0:T(1,128)S(1)} async-done(((f32[4,1,2048]{2,1,0:T(1,128)}), f32[4,1,2048]{2,1,0:T(1,128)S(1)}, u32[]{:S(2)}, u32[]{:S(2)}) %all-to-all-start.10) | async-done | bytes 32800 | tf_op jit(solution)/shard_map/all_to_all | solution.py:178
  218.1 3.3 %all-to-all-start.11 = ((f32[4,4,256]{2,0,1:T(4,128)}), f32[4,4,256]{2,0,1:T(4,128)S(1)}, u32[]{:S(2)}, u32[]{:S(2)}) async-start(f32[4,4,256]{2,0,1:T(4,128)} %copy.299), calls=%async_computation.11 | async-start | bytes 32768 | tf_op jit(solution)/shard_map/all_to_all | solution.py:181
  222.2 4.7 %all-to-all-done.11 = f32[4,4,256]{2,0,1:T(4,128)S(1)} async-done(((f32[4,4,256]{2,0,1:T(4,128)}), f32[4,4,256]{2,0,1:T(4,128)S(1)}, u32[]{:S(2)}, u32[]{:S(2)}) %all-to-all-start.11) | async-done | bytes 16416 | tf_op jit(solution)/shard_map/all_to_all | solution.py:181
  (236 shorter events, 62.9 us)
Async XLA Ops:
  0.6 12.7 %copy-start.5 = (bf16[65,32,128]{2,1,0:T(8,128)(2,1)S(1)}, bf16[65,32,128]{2,1,0:T(8,128)(2,1)}, u32[]{:S(2)}) copy-start(bf16[65,32,128]{2,1,0:T(8,128)(2,1)} %param.25) | copy-start | bytes 1597444
  1.9 12.4 %copy-start = (f32[64,2,32,128]{3,2,1,0:T(8,128)S(1)}, f32[64,2,32,128]{3,2,1,0:T(8,128)}, u32[]{:S(2)}) copy-start(f32[64,2,32,128]{3,2,1,0:T(8,128)} %param.24) | copy-start | bytes 6291460
  2.0 14.1 %collective-permute-start.2 = (f32[12,16,2]{2,1,0:T(8,128)S(1)}, f32[12,16,2]{2,1,0:T(8,128)S(1)}, u32[]{:S(2)}, u32[]{:S(2)}) collective-permute-start(f32[12,16,2]{2,1,0:T(8,128)S(1)} %get-tuple-element.33), channel_id=1, source_target_pairs={{1,0},{2,1},{3,2},{0,3},{5,4},{6,5},{7,6},{4,7},{9,8},{10,9},{11,1... | collective-permute-start | bytes 4616 | tf_op jit(solution)/shard_map/ppermute | solution.py:29
  7.1 9.0 %collective-permute-start.3 = (f32[12,16,2]{2,1,0:T(8,128)S(1)}, f32[12,16,2]{2,1,0:T(8,128)S(1)}, u32[]{:S(2)}, u32[]{:S(2)}) collective-permute-start(f32[12,16,2]{2,1,0:T(8,128)S(1)} %get-tuple-element.34), channel_id=1, source_target_pairs={{0,1},{1,2},{2,3},{3,0},{4,5},{5,6},{6,7},{7,4},{8,9},{9,10},{10,1... | collective-permute-start | bytes 4616 | tf_op jit(solution)/shard_map/ppermute | solution.py:26
  7.1 9.0 %collective-permute-start = (f32[12,2,256]{2,1,0:T(2,128)S(1)}, f32[12,2,256]{2,1,0:T(2,128)S(1)}, u32[]{:S(2)}, u32[]{:S(2)}) collective-permute-start(f32[12,2,256]{2,1,0:T(2,128)S(1)} %get-tuple-element.31), channel_id=1, source_target_pairs={{4,0},{8,4},{12,8},{16,12},{20,16},{24,20},{28,24},{0,28},{5,1},{9... | collective-permute-start | bytes 73736 | tf_op jit(solution)/shard_map/ppermute | solution.py:29
  8.8 7.3 %collective-permute-start.1 = (f32[12,2,256]{2,1,0:T(2,128)S(1)}, f32[12,2,256]{2,1,0:T(2,128)S(1)}, u32[]{:S(2)}, u32[]{:S(2)}) collective-permute-start(f32[12,2,256]{2,1,0:T(2,128)S(1)} %get-tuple-element.32), channel_id=1, source_target_pairs={{0,4},{4,8},{8,12},{12,16},{16,20},{20,24},{24,28},{28,0},{1,5},{5... | collective-permute-start | bytes 73736 | tf_op jit(solution)/shard_map/ppermute | solution.py:26
  14.1 1.9 copy-start.11
  14.1 2.0 copy-start.22
  14.1 2.0 copy-start.31
  14.3 14.1 %copy-start.2 = (f32[12,16,256]{2,1,0:T(8,128)S(1)}, f32[12,16,256]{2,1,0:T(8,128)}, u32[]{:S(2)}) copy-start(f32[12,16,256]{2,1,0:T(8,128)} %param.15) | copy-start | bytes 589828
  17.1 11.3 %collective-permute-start.4 = (f32[12,2,256]{2,1,0:T(2,128)}, f32[12,2,256]{2,1,0:T(2,128)}, u32[]{:S(2)}, u32[]{:S(2)}) collective-permute-start(f32[12,2,256]{2,1,0:T(2,128)} %get-tuple-element.30), channel_id=1, source_target_pairs={{4,0},{8,4},{12,8},{16,12},{20,16},{24,20},{28,24},{0,28},{5,1},{9... | collective-permute-start | bytes 73736 | tf_op jit(solution)/shard_map/ppermute | solution.py:29
  19.8 8.6 %collective-permute-start.5 = (f32[12,2,256]{2,1,0:T(2,128)}, f32[12,2,256]{2,1,0:T(2,128)}, u32[]{:S(2)}, u32[]{:S(2)}) collective-permute-start(f32[12,2,256]{2,1,0:T(2,128)} %get-tuple-element.29), channel_id=1, source_target_pairs={{0,4},{4,8},{8,12},{12,16},{16,20},{20,24},{24,28},{28,0},{1,5},{5... | collective-permute-start | bytes 73736 | tf_op jit(solution)/shard_map/ppermute | solution.py:26
  30.4 0.7 copy-start.6
  33.8 13.6 %all-to-all-start = ((f32[4,4,256]{2,1,0:T(4,128)}), f32[4,4,256]{2,1,0:T(4,128)}, u32[]{:S(2)}, u32[]{:S(2)}) async-start(f32[4,4,256]{2,1,0:T(4,128)} %all_to_all.144), calls=%async_computation | async-start | bytes 32768 | tf_op jit(solution)/shard_map/all_to_all | solution.py:152
  40.2 26.6 %collective-permute-start.8 = (f32[12,20,2]{2,1,0:T(8,128)}, f32[12,20,2]{2,1,0:T(8,128)}, u32[]{:S(2)}, u32[]{:S(2)}) collective-permute-start(f32[12,20,2]{2,1,0:T(8,128)} %get-tuple-element.21), channel_id=1, source_target_pairs={{1,0},{2,1},{3,2},{0,3},{5,4},{6,5},{7,6},{4,7},{9,8},{10,9},{11,1... | collective-permute-start | bytes 5768 | tf_op jit(solution)/shard_map/ppermute | solution.py:29
  44.0 22.8 %collective-permute-start.9 = (f32[12,20,2]{2,1,0:T(8,128)}, f32[12,20,2]{2,1,0:T(8,128)}, u32[]{:S(2)}, u32[]{:S(2)}) collective-permute-start(f32[12,20,2]{2,1,0:T(8,128)} %get-tuple-element.22), channel_id=1, source_target_pairs={{0,1},{1,2},{2,3},{3,0},{4,5},{5,6},{6,7},{7,4},{8,9},{9,10},{10,1... | collective-permute-start | bytes 5768 | tf_op jit(solution)/shard_map/ppermute | solution.py:26
  45.6 50.5 %collective-permute-start.6 = (f32[12,2,256]{2,1,0:T(2,128)}, f32[12,2,256]{2,1,0:T(2,128)}, u32[]{:S(2)}, u32[]{:S(2)}) collective-permute-start(f32[12,2,256]{2,1,0:T(2,128)} %get-tuple-element.25), channel_id=1, source_target_pairs={{4,0},{8,4},{12,8},{16,12},{20,16},{24,20},{28,24},{0,28},{5,1},{9... | collective-permute-start | bytes 73736 | tf_op jit(solution)/shard_map/ppermute | solution.py:29
  47.4 48.7 %collective-permute-start.7 = (f32[12,2,256]{2,1,0:T(2,128)}, f32[12,2,256]{2,1,0:T(2,128)}, u32[]{:S(2)}, u32[]{:S(2)}) collective-permute-start(f32[12,2,256]{2,1,0:T(2,128)} %get-tuple-element.26), channel_id=1, source_target_pairs={{0,4},{4,8},{8,12},{12,16},{16,20},{20,24},{24,28},{28,0},{1,5},{5... | collective-permute-start | bytes 73736 | tf_op jit(solution)/shard_map/ppermute | solution.py:26
  51.4 2.5 %copy-start.7 = (f32[4,32,32]{1,2,0:T(8,128)}, f32[4,32,32]{1,2,0:T(8,128)S(1)}, u32[]{:S(2)}) copy-start(f32[4,32,32]{1,2,0:T(8,128)S(1)} %fusion.42) | copy-start | bytes 49156
  52.6 1.3 copy-start.8
  62.9 8.9 %all-to-all-start.1 = ((f32[8,1,1024]{2,1,0:T(1,128)}), f32[8,1,1024]{2,1,0:T(1,128)}, u32[]{:S(2)}, u32[]{:S(2)}) async-start(f32[8,1,1024]{2,1,0:T(1,128)} %reshape.360), calls=%async_computation.1 | async-start | bytes 65536 | tf_op jit(solution)/shard_map/all_to_all | solution.py:160
  69.3 19.9 %copy-start.18 = (bf16[1,32,128]{1,2,0:T(8,128)(2,1)S(1)}, bf16[1,32,128]{1,2,0:T(8,128)(2,1)}, u32[]{:S(2)}) copy-start(bf16[1,32,128]{1,2,0:T(8,128)(2,1)} %copy.324) | copy-start | bytes 24580
  74.8 10.6 %all-to-all-start.2 = ((f32[4,1,2048]{2,1,0:T(1,128)}), f32[4,1,2048]{2,1,0:T(1,128)S(1)}, u32[]{:S(2)}, u32[]{:S(2)}) async-start(f32[4,1,2048]{2,1,0:T(1,128)} %reshape.362), calls=%async_computation.2 | async-start | bytes 65536 | tf_op jit(solution)/shard_map/all_to_all | solution.py:161
  81.3 14.8 %collective-permute-start.10 = (f32[12,16,2]{2,1,0:T(8,128)}, f32[12,16,2]{2,1,0:T(8,128)}, u32[]{:S(2)}, u32[]{:S(2)}) collective-permute-start(f32[12,16,2]{2,1,0:T(8,128)} %get-tuple-element.27), channel_id=1, source_target_pairs={{1,0},{2,1},{3,2},{0,3},{5,4},{6,5},{7,6},{4,7},{9,8},{10,9},{11,1... | collective-permute-start | bytes 4616 | tf_op jit(solution)/shard_map/ppermute | solution.py:29
  85.1 11.0 %collective-permute-start.11 = (f32[12,16,2]{2,1,0:T(8,128)}, f32[12,16,2]{2,1,0:T(8,128)}, u32[]{:S(2)}, u32[]{:S(2)}) collective-permute-start(f32[12,16,2]{2,1,0:T(8,128)} %get-tuple-element.28), channel_id=1, source_target_pairs={{0,1},{1,2},{2,3},{3,0},{4,5},{5,6},{6,7},{7,4},{8,9},{9,10},{10,1... | collective-permute-start | bytes 4616 | tf_op jit(solution)/shard_map/ppermute | solution.py:26
  86.3 2.9 %copy-start.20 = (f32[1,32,128]{1,2,0:T(8,128)S(1)}, f32[1,32,128]{1,2,0:T(8,128)}, u32[]{:S(2)}) copy-start(f32[1,32,128]{1,2,0:T(8,128)} %copy.214) | copy-start | bytes 49156
  86.3 2.9 %copy-start.21 = (f32[1,32,128]{1,2,0:T(8,128)S(1)}, f32[1,32,128]{1,2,0:T(8,128)}, u32[]{:S(2)}) copy-start(f32[1,32,128]{1,2,0:T(8,128)} %copy.233) | copy-start | bytes 49156
  86.3 3.7 %copy-start.24 = (f32[8,16]{0,1:T(8,128)S(1)}, f32[8,16]{0,1:T(8,128)}, u32[]{:S(2)}) copy-start(f32[8,16]{0,1:T(8,128)} %get-tuple-element.61) | copy-start | bytes 1540
  86.3 3.7 %copy-start.26 = (f32[8,16]{0,1:T(8,128)S(1)}, f32[8,16]{0,1:T(8,128)}, u32[]{:S(2)}) copy-start(f32[8,16]{0,1:T(8,128)} %get-tuple-element.62) | copy-start | bytes 1540
  88.8 2.5 %copy-start.12 = (f32[32,16,8]{0,2,1:T(8,128)}, f32[32,16,8]{0,2,1:T(8,128)S(1)}, u32[]{:S(2)}) copy-start(f32[32,16,8]{0,2,1:T(8,128)S(1)} %copy.236) | copy-start | bytes 49156
  89.1 0.8 copy-start.14
  92.1 8.8 %all-to-all-start.3 = ((f32[8,1,1024]{2,1,0:T(1,128)}), f32[8,1,1024]{2,1,0:T(1,128)}, u32[]{:S(2)}, u32[]{:S(2)}) async-start(f32[8,1,1024]{2,1,0:T(1,128)} %reshape.364), calls=%async_computation.3 | async-start | bytes 65536 | tf_op jit(solution)/shard_map/all_to_all | solution.py:177
  98.8 109.7 %copy-start.1 = (f32[12,16,256]{2,1,0:T(8,128)}, f32[12,16,256]{2,1,0:T(8,128)S(1)}, u32[]{:S(2)}) copy-start(f32[12,16,256]{2,1,0:T(8,128)S(1)} %fusion.64) | copy-start | bytes 589828
  98.8 47.1 %copy-start.3 = (f32[12,16,256]{2,1,0:T(8,128)S(1)}, f32[12,16,256]{2,1,0:T(8,128)}, u32[]{:S(2)}) copy-start(f32[12,16,256]{2,1,0:T(8,128)} %param.15) | copy-start | bytes 589828
  107.8 10.6 %all-to-all-start.4 = ((f32[4,1,2048]{2,1,0:T(1,128)}), f32[4,1,2048]{2,1,0:T(1,128)}, u32[]{:S(2)}, u32[]{:S(2)}) async-start(f32[4,1,2048]{2,1,0:T(1,128)} %reshape.366), calls=%async_computation.4 | async-start | bytes 65536 | tf_op jit(solution)/shard_map/all_to_all | solution.py:178
  113.3 32.5 %collective-permute-start.12 = (f32[12,2,256]{2,1,0:T(2,128)}, f32[12,2,256]{2,1,0:T(2,128)}, u32[]{:S(2)}, u32[]{:S(2)}) collective-permute-start(f32[12,2,256]{2,1,0:T(2,128)} %get-tuple-element.24), channel_id=1, source_target_pairs={{4,0},{8,4},{12,8},{16,12},{20,16},{24,20},{28,24},{0,28},{5,1},{9... | collective-permute-start | bytes 73736 | tf_op jit(solution)/shard_map/ppermute | solution.py:29
  113.5 32.3 %collective-permute-start.13 = (f32[12,2,256]{2,1,0:T(2,128)}, f32[12,2,256]{2,1,0:T(2,128)}, u32[]{:S(2)}, u32[]{:S(2)}) collective-permute-start(f32[12,2,256]{2,1,0:T(2,128)} %get-tuple-element.23), channel_id=1, source_target_pairs={{0,4},{4,8},{8,12},{12,16},{16,20},{20,24},{24,28},{28,0},{1,5},{5... | collective-permute-start | bytes 73736 | tf_op jit(solution)/shard_map/ppermute | solution.py:26
  142.0 9.5 %all-to-all-start.5 = ((f32[4,4,256]{2,0,1:T(4,128)}), f32[4,4,256]{2,0,1:T(4,128)}, u32[]{:S(2)}, u32[]{:S(2)}) async-start(f32[4,4,256]{2,0,1:T(4,128)} %copy.258), calls=%async_computation.5 | async-start | bytes 32768 | tf_op jit(solution)/shard_map/all_to_all | solution.py:181
  155.6 9.5 %all-to-all-start.6 = ((f32[4,4,256]{2,1,0:T(4,128)}), f32[4,4,256]{2,1,0:T(4,128)}, u32[]{:S(2)}, u32[]{:S(2)}) async-start(f32[4,4,256]{2,1,0:T(4,128)} %all_to_all.164), calls=%async_computation.6 | async-start | bytes 32768 | tf_op jit(solution)/shard_map/all_to_all | solution.py:152
  160.5 13.3 %copy-start.23 = (f32[2,32,128]{2,1,0:T(8,128)S(1)}, f32[2,32,128]{2,1,0:T(8,128)}, u32[]{:S(2)}) copy-start(f32[2,32,128]{2,1,0:T(8,128)} %multiply_reduce_fusion.1) | copy-start | bytes 98308
  160.5 13.6 %copy-start.30 = (bf16[1,32,128]{2,1,0:T(8,128)(2,1)S(1)}, bf16[1,32,128]{2,1,0:T(8,128)(2,1)}, u32[]{:S(2)}) copy-start(bf16[1,32,128]{2,1,0:T(8,128)(2,1)} %get-tuple-element.15) | copy-start | bytes 24580
  169.2 21.8 %copy-start.28 = (f32[8,16]{0,1:T(8,128)S(1)}, f32[8,16]{0,1:T(8,128)}, u32[]{:S(2)}) copy-start(f32[8,16]{0,1:T(8,128)} %get-tuple-element.59) | copy-start | bytes 1540
  169.2 21.8 %copy-start.29 = (f32[8,16]{0,1:T(8,128)S(1)}, f32[8,16]{0,1:T(8,128)}, u32[]{:S(2)}) copy-start(f32[8,16]{0,1:T(8,128)} %get-tuple-element.60) | copy-start | bytes 1540
  170.5 8.1 %all-to-all-start.7 = ((f32[8,1,1024]{2,1,0:T(1,128)}), f32[8,1,1024]{2,1,0:T(1,128)S(1)}, u32[]{:S(2)}, u32[]{:S(2)}) async-start(f32[8,1,1024]{2,1,0:T(1,128)} %reshape.368), calls=%async_computation.7 | async-start | bytes 65536 | tf_op jit(solution)/shard_map/all_to_all | solution.py:160
  173.8 18.5 %copy-start.13 = (f32[32,16,8]{0,2,1:T(8,128)S(1)}, f32[32,16,8]{0,2,1:T(8,128)}, u32[]{:S(2)}) copy-start(f32[32,16,8]{0,2,1:T(8,128)} %copy-done.12) | copy-start | bytes 49156
  173.8 18.5 %copy-start.15 = (f32[32,16,8]{0,2,1:T(8,128)S(1)}, f32[32,16,8]{0,2,1:T(8,128)}, u32[]{:S(2)}) copy-start(f32[32,16,8]{0,2,1:T(8,128)} %copy-done.14) | copy-start | bytes 49156
  173.8 18.5 %copy-start.19 = (bf16[1,32,128]{1,2,0:T(8,128)(2,1)S(1)}, bf16[1,32,128]{1,2,0:T(8,128)(2,1)}, u32[]{:S(2)}) copy-start(bf16[1,32,128]{1,2,0:T(8,128)(2,1)} %copy.324) | copy-start | bytes 24580
  180.3 12.9 %copy-start.25 = (f32[8,16]{0,1:T(8,128)S(1)}, f32[8,16]{0,1:T(8,128)}, u32[]{:S(2)}) copy-start(f32[8,16]{0,1:T(8,128)} %get-tuple-element.61) | copy-start | bytes 1540
  180.3 12.9 %copy-start.27 = (f32[8,16]{0,1:T(8,128)S(1)}, f32[8,16]{0,1:T(8,128)}, u32[]{:S(2)}) copy-start(f32[8,16]{0,1:T(8,128)} %get-tuple-element.62) | copy-start | bytes 1540
  180.3 9.0 %all-to-all-start.8 = ((f32[4,1,2048]{2,1,0:T(1,128)}), f32[4,1,2048]{2,1,0:T(1,128)S(1)}, u32[]{:S(2)}, u32[]{:S(2)}) async-start(f32[4,1,2048]{2,1,0:T(1,128)} %reshape.370), calls=%async_computation.8 | async-start | bytes 65536 | tf_op jit(solution)/shard_map/all_to_all | solution.py:161
  192.3 16.1 %copy-start.4 = (f32[12,16,256]{2,1,0:T(8,128)S(1)}, f32[12,16,256]{2,1,0:T(8,128)}, u32[]{:S(2)}) copy-start(f32[12,16,256]{2,1,0:T(8,128)} %fusion.128) | copy-start | bytes 589828
  195.3 8.1 %all-to-all-start.9 = ((f32[8,1,1024]{2,1,0:T(1,128)}), f32[8,1,1024]{2,1,0:T(1,128)S(1)}, u32[]{:S(2)}, u32[]{:S(2)}) async-start(f32[8,1,1024]{2,1,0:T(1,128)} %reshape.372), calls=%async_computation.9 | async-start | bytes 65536 | tf_op jit(solution)/shard_map/all_to_all | solution.py:177
  198.7 17.9 %copy-start.16 = (f32[32,32]{0,1:T(8,128)S(1)}, f32[32,32]{0,1:T(8,128)}, u32[]{:S(2)}) copy-start(f32[32,32]{0,1:T(8,128)} %copy.251) | copy-start | bytes 12292
  198.7 17.9 %copy-start.17 = (f32[32,32]{0,1:T(8,128)S(1)}, f32[32,32]{0,1:T(8,128)}, u32[]{:S(2)}) copy-start(f32[32,32]{0,1:T(8,128)} %copy.254) | copy-start | bytes 12292
  198.8 9.6 %collective-permute-start.14 = (f32[12,20,2]{2,1,0:T(8,128)S(1)}, f32[12,20,2]{2,1,0:T(8,128)S(1)}, u32[]{:S(2)}, u32[]{:S(2)}) collective-permute-start(f32[12,20,2]{2,1,0:T(8,128)S(1)} %get-tuple-element.19), channel_id=1, source_target_pairs={{1,0},{2,1},{3,2},{0,3},{5,4},{6,5},{7,6},{4,7},{9,8},{10,9},{11,1... | collective-permute-start | bytes 5768 | tf_op jit(solution)/shard_map/ppermute | solution.py:29
  199.5 8.9 %collective-permute-start.15 = (f32[12,20,2]{2,1,0:T(8,128)S(1)}, f32[12,20,2]{2,1,0:T(8,128)S(1)}, u32[]{:S(2)}, u32[]{:S(2)}) collective-permute-start(f32[12,20,2]{2,1,0:T(8,128)S(1)} %get-tuple-element.20), channel_id=1, source_target_pairs={{0,1},{1,2},{2,3},{3,0},{4,5},{5,6},{6,7},{7,4},{8,9},{9,10},{10,1... | collective-permute-start | bytes 5768 | tf_op jit(solution)/shard_map/ppermute | solution.py:26
  204.3 17.0 %copy-start.9 = (f32[12,16,256]{2,1,0:T(8,128)S(1)}, f32[12,16,256]{2,1,0:T(8,128)}, u32[]{:S(2)}) copy-start(f32[12,16,256]{2,1,0:T(8,128)} %get-tuple-element.18) | copy-start | bytes 589828
  204.4 17.0 %copy-start.10 = (f32[1,12,16,256]{3,2,1,0:T(8,128)S(1)}, f32[1,12,16,256]{3,2,1,0:T(8,128)}, u32[]{:S(2)}) copy-start(f32[1,12,16,256]{3,2,1,0:T(8,128)} %get-tuple-element.17) | copy-start | bytes 589828
  205.2 8.9 %all-to-all-start.10 = ((f32[4,1,2048]{2,1,0:T(1,128)}), f32[4,1,2048]{2,1,0:T(1,128)S(1)}, u32[]{:S(2)}, u32[]{:S(2)}) async-start(f32[4,1,2048]{2,1,0:T(1,128)} %reshape.374), calls=%async_computation.10 | async-start | bytes 65536 | tf_op jit(solution)/shard_map/all_to_all | solution.py:178
  218.1 8.8 %all-to-all-start.11 = ((f32[4,4,256]{2,0,1:T(4,128)}), f32[4,4,256]{2,0,1:T(4,128)S(1)}, u32[]{:S(2)}, u32[]{:S(2)}) async-start(f32[4,4,256]{2,0,1:T(4,128)} %copy.299), calls=%async_computation.11 | async-start | bytes 32768 | tf_op jit(solution)/shard_map/all_to_all | solution.py:181
where the time goes:
time: 231 us; the launch traced here: 228 us
  starting transfers between devices  68.1 us (29%)
  local copies, waits for them, and re-layouts  56.4 us (24%)
  waiting for transfers between devices  38.5 us (17%)
  other arithmetic  32.7 us (14%)
  matrix products  29.9 us (13%)
    dot_general x58, matrix products, contract(): return jnp.einsum(form, left, right, precision=lax.Precision.HIGHEST)  29.9 us
    ppermute x8, starting transfers between devices, padded_2(): lax.ppermute(lax.slice_in_dim(block, 0, width, axis=dim), axis, backward)  19.8 us
    unnamed x84, local copies, waits for them, and re-layouts  15.5 us
    all_to_all x2, waiting for transfers between devices, body(): lax.all_to_all(partway, 'dip', split_axis=5, concat_axis=2, tiled=True)  8.79 us
    all_to_all x2, starting transfers between devices, body(): lines = lax.all_to_all(slip, 'dip', split_axis=0, concat_axis=1, tiled=True)  8.66 us
    all_to_all x2, waiting for transfers between devices, body(): lax.all_to_all(field_real, 'dip', split_axis=1, concat_axis=0, tiled=True)  8.31 us
    all_to_all x2, starting transfers between devices, body(): lax.all_to_all(halfway, 'dip', split_axis=2, concat_axis=5, tiled=True)  8.2 us
    all_to_all x2, starting transfers between devices, body(): lax.all_to_all(partway, 'dip', split_axis=5, concat_axis=2, tiled=True)  8.11 us
  transfers between devices with their start and end apart: 28, of which 11 were waited for; matrix products, arithmetic and copies ran while one was open for 36% of the time, Pallas kernels for 0%

commit v1 on v0

--- a/solution.py
+++ b/solution.py
@@ -1,8 +1,12 @@
+import functools
 import math
 
 import jax
 import jax.numpy as jnp
+import numpy as np
 from jax import lax
+from jax.experimental import pallas as pl
+from jax.experimental.pallas import tpu as pltpu
 from jax.sharding import PartitionSpec as P
 
 STEPS = 2
@@ -106,7 +110,7 @@
     return (out_real, out_imag)
 
 
-def body(
+def general_body(
     velocity,
     stress,
     shear_modulus,
@@ -182,6 +186,608 @@
     return (velocity, jnp.stack([stress_x, stress_y, stress_z]), slip, traction, functional)
 
 
+LANES = 128
+SUBLANES = 8
+MESH = pl.DeviceIdType.MESH
+
+
+def split_bf16(value):
+    high = value.astype(jnp.bfloat16)
+    return high, (value - high.astype(jnp.float32)).astype(jnp.bfloat16)
+
+
+def split_table(table):
+    table = np.asarray(table, np.float32)
+    high = table.astype(jnp.bfloat16)
+    return high, (table - high.astype(np.float32)).astype(jnp.bfloat16)
+
+
+def strike_table(total_x):
+    index = np.arange(total_x)
+    angle = 2.0 * np.pi / total_x * (index[:, None] * index[None, :] % total_x)
+    return np.concatenate([np.cos(angle), np.sin(angle)], axis=1) / np.sqrt(total_x)
+
+
+def dip_table(strike_count, group, modes, cols, total_y):
+    freq = (np.arange(strike_count)[:, None] * modes + np.arange(group)[None, :])[..., None]
+    angle = 2.0 * np.pi / cols * (freq * np.arange(cols) % cols)
+    cos, sin = np.cos(angle), np.sin(angle)
+    top = np.concatenate([cos, sin], axis=-1)
+    bottom = np.concatenate([-sin, cos], axis=-1)
+    table = np.stack([top, bottom], axis=1)
+    return table.reshape(strike_count * 2 * group, 2 * cols) / np.sqrt(total_y)
+
+
+def twiddle_table(dip_count, modes, cols, total_y):
+    freq = np.arange(dip_count)[:, None] * modes + np.arange(dip_count)[None, :]
+    angle = 2.0 * np.pi / total_y * (freq[..., None] * np.arange(cols) % total_y)
+    return np.stack([np.cos(angle), -np.sin(angle)], axis=1).astype(np.float32)
+
+
+def dot3(left, right_high, right_low):
+    high, low = split_bf16(left)
+    rows = left.shape[0]
+    both = jnp.dot(
+        jnp.concatenate([high, low], axis=0), right_high, preferred_element_type=jnp.float32
+    )
+    return both[:rows] + both[rows:] + jnp.dot(high, right_low, preferred_element_type=jnp.float32)
+
+
+def dot3_nt(left_high, left_low, right):
+    high, low = split_bf16(right)
+
+    def product(a, b):
+        return lax.dot_general(a, b, (((1,), (1,)), ((), ())), preferred_element_type=jnp.float32)
+
+    return product(left_high, high) + product(left_high, low) + product(left_low, high)
+
+
+def rupture_kernel(
+    strike_count,
+    dip_count,
+    vel_in,
+    stress_in,
+    shear,
+    buoy,
+    prestress,
+    normal_stress,
+    crit_slip,
+    slip_in,
+    traction_in,
+    functional_in,
+    flags,
+    hist,
+    kern,
+    dip_hi,
+    dip_lo,
+    strike_hi,
+    strike_lo,
+    twiddle,
+    vel,
+    stress,
+    slip_out,
+    traction_out,
+    functional_out,
+    padded,
+    edge_x,
+    edge_y,
+    halo_x,
+    halo_y,
+    slip_buf,
+    gathered,
+    send_b,
+    recv_b,
+    send_c,
+    recv_c,
+    send_d,
+    recv_d,
+    stored,
+    weights,
+    edge_sem,
+    halo_sem,
+    a_send,
+    a_recv,
+    b_send,
+    b_recv,
+    c_send,
+    c_recv,
+    d_send,
+    d_recv,
+):
+    depth, rows, cols = vel_in.shape
+    modes = hist.shape[2]
+    total_x = hist.shape[3]
+    stored_count = hist.shape[0]
+    group = modes // dip_count
+    my_s = lax.axis_index("strike")
+    my_d = lax.axis_index("dip")
+
+    def ring(me, offset, count):
+        return lax.rem(me + offset + count, count)
+
+    def remote(src, dst, send_sem, recv_sem, axis, target):
+        return pltpu.make_async_remote_copy(
+            src_ref=src,
+            dst_ref=dst,
+            send_sem=send_sem,
+            recv_sem=recv_sem,
+            device_id={axis: target},
+            device_id_type=MESH,
+        )
+
+    lane = lax.broadcasted_iota(jnp.int32, (rows, LANES), 1)
+    column = lax.broadcasted_iota(jnp.int32, (rows, cols), 1)
+    lane_b = lax.broadcasted_iota(jnp.int32, (2 * group, LANES), 1) // rows
+
+    def pack_x(turn, field):
+        edge_x[turn, 0] = field[:, rows - 2 : rows, :]
+        edge_x[turn, 1] = field[:, 0:2, :]
+
+    def pack_y(turn, layer):
+        low = jnp.zeros((rows, LANES), jnp.float32)
+        high = jnp.zeros((rows, LANES), jnp.float32)
+        for z in range(depth):
+            here = lane // 2 == z
+            last = layer(z)[:, cols - LANES :]
+            first = layer(z)[:, :LANES]
+            low = jnp.where(here, pltpu.roll(last, (2 * z + 2) % LANES, 1), low)
+            high = jnp.where(here, pltpu.roll(first, 2 * z, 1) if z else first, high)
+        edge_y[turn, 0] = low
+        edge_y[turn, 1] = high
+
+    def halo_copies(turn):
+        copies = []
+        for side, step in ((0, 1), (1, -1)):
+            copies.append(
+                remote(
+                    edge_x.at[turn, side],
+                    halo_x.at[turn, side],
+                    edge_sem.at[turn, side],
+                    halo_sem.at[turn, side],
+                    "strike",
+                    ring(my_s, step, strike_count),
+                )
+            )
+            copies.append(
+                remote(
+                    edge_y.at[turn, side],
+                    halo_y.at[turn, side],
+                    edge_sem.at[turn, side + 2],
+                    halo_sem.at[turn, side + 2],
+                    "dip",
+                    ring(my_d, step, dip_count),
+                )
+            )
+        return copies
+
+    def start_halos(turn):
+        copies = halo_copies(turn)
+        for copy in copies:
+            copy.start()
+        return copies
+
+    def wait_halos(copies):
+        for copy in copies:
+            copy.wait_recv()
+
+    def fill_padded(turn, field):
+        padded[:, SUBLANES : SUBLANES + rows, :] = field[...]
+        padded[:, SUBLANES - 2 : SUBLANES, :] = halo_x[turn, 0]
+        padded[:, SUBLANES + rows : SUBLANES + rows + 2, :] = halo_x[turn, 1]
+
+    def diff_x(z):
+        def window(offset):
+            return padded[z, SUBLANES + offset : SUBLANES + offset + rows, :]
+
+        return coef_near * (window(1) - window(-1)) + coef_far * (window(2) - window(-2))
+
+    def diff_y(turn, z, field):
+        low = halo_y[turn, 0]
+        high = halo_y[turn, 1]
+        low_0, low_1 = low[:, 2 * z : 2 * z + 1], low[:, 2 * z + 1 : 2 * z + 2]
+        high_0, high_1 = high[:, 2 * z : 2 * z + 1], high[:, 2 * z + 1 : 2 * z + 2]
+        back_1 = jnp.where(column == 0, low_1, pltpu.roll(field, 1, 1))
+        back_2 = jnp.where(
+            column == 0, low_0, jnp.where(column == 1, low_1, pltpu.roll(field, 2, 1))
+        )
+        next_1 = jnp.where(column == cols - 1, high_0, pltpu.roll(field, cols - 1, 1))
+        next_2 = jnp.where(
+            column == cols - 2,
+            high_0,
+            jnp.where(column == cols - 1, high_1, pltpu.roll(field, cols - 2, 1)),
+        )
+        return coef_near * (next_1 - back_1) + coef_far * (next_2 - back_2)
+
+    def diff_z(z, layer, ghost):
+        def at(index):
+            if index < 0:
+                return ghost
+            return layer(index) if index < depth else None
+
+        total = None
+        for offset, coef in ((1, coef_near), (-1, -coef_near), (2, coef_far), (-2, -coef_far)):
+            value = at(z + offset)
+            if value is not None:
+                total = coef * value if total is None else total + coef * value
+        return total
+
+    def velocity_layer(turn, z, source, stress_ref, traction):
+        divergence = (
+            diff_x(z)
+            + diff_y(turn, z, stress_ref[1, z])
+            + diff_z(z, lambda i: stress_ref[2, i], traction)
+        )
+        vel[z] = source[z] + courant * buoy[z] * divergence
+
+    def stress_z_layer(z, stress_ref):
+        return stress_ref[2, z] + courant * shear[z] * diff_z(z, lambda i: vel[i], None)
+
+    def stress_layers(turn, stress_ref):
+        fill_padded(turn, vel)
+        for z in range(depth):
+            modulus = courant * shear[z]
+            stress[0, z] = stress_ref[0, z] + modulus * diff_x(z)
+            stress[1, z] = stress_ref[1, z] + modulus * diff_y(turn, z, vel[z])
+            stress[2, z] = stress_z_layer(z, stress_ref)
+
+    def start_gather(step, value):
+        slip_buf[step] = value
+        gathered[step, my_d] = value
+        copies = []
+        for k in range(1, dip_count):
+            copy = remote(
+                slip_buf.at[step],
+                gathered.at[step, my_d],
+                a_send.at[step, k],
+                a_recv.at[step, k],
+                "dip",
+                ring(my_d, k, dip_count),
+            )
+            copy.start()
+            copies.append(copy)
+        return copies
+
+    def wait_gather(step):
+        for k in range(1, dip_count):
+            source = ring(my_d, -k, dip_count)
+            remote(
+                slip_buf.at[step],
+                gathered.at[step, source],
+                a_send.at[step, k],
+                a_recv.at[step, k],
+                "dip",
+                source,
+            ).wait_recv()
+
+    def exchange_start(step, axis, me, count, send, recv, send_sem, recv_sem):
+        recv[step, me] = send[step, me]
+        copies = []
+        for k in range(1, count):
+            target = ring(me, k, count)
+            copy = remote(
+                send.at[step, target],
+                recv.at[step, me],
+                send_sem.at[step, k],
+                recv_sem.at[step, k],
+                axis,
+                target,
+            )
+            copy.start()
+            copies.append(copy)
+        return copies
+
+    def exchange_wait(step, axis, me, count, send, recv, send_sem, recv_sem):
+        for k in range(1, count):
+            source = ring(me, -k, count)
+            remote(
+                send.at[step, source],
+                recv.at[step, source],
+                send_sem.at[step, k],
+                recv_sem.at[step, k],
+                axis,
+                source,
+            ).wait_recv()
+
+    def phase(k0, dy):
+        angle = 2.0 * math.pi * (k0 * dy % dip_count) / dip_count
+        return round(math.cos(angle), 15), round(math.sin(angle), 15)
+
+    def weighted(terms):
+        total = None
+        for coef, value in terms:
+            if abs(coef) < 1e-12:
+                continue
+            term = value if coef == 1.0 else (-value if coef == -1.0 else coef * value)
+            total = term if total is None else total + term
+        return jnp.zeros((rows, cols), jnp.float32) if total is None else total
+
+    def dip_forward(step):
+        parts = [gathered[step, i] for i in range(dip_count)]
+        real, imag = [], []
+        for k0 in range(dip_count):
+            phases = [phase(k0, dy) for dy in range(dip_count)]
+            u_re = weighted([(c, part) for (c, _), part in zip(phases, parts)])
+            u_im = weighted([(-s, part) for (_, s), part in zip(phases, parts)])
+            t_re = twiddle[my_d, 0, k0 : k0 + 1, :]
+            t_im = twiddle[my_d, 1, k0 : k0 + 1, :]
+            real.append(u_re * t_re - u_im * t_im)
+            imag.append(u_re * t_im + u_im * t_re)
+        spare = LANES - dip_count * rows
+        if spare:
+            real.append(jnp.zeros((spare, cols), jnp.float32))
+            imag.append(jnp.zeros((spare, cols), jnp.float32))
+        both = jnp.concatenate(
+            [jnp.concatenate(real, axis=0), jnp.concatenate(imag, axis=0)], axis=1
+        )
+        out = dot3_nt(dip_hi[...], dip_lo[...], both)
+        send_b[step] = out.reshape(strike_count, 2 * group, LANES)
+
+    def strike_forward(step):
+        blocks = []
+        for k0 in range(dip_count):
+            block = jnp.zeros((2 * group, LANES), jnp.float32)
+            for s in range(strike_count):
+                shift = rows * (s - k0) % LANES
+                piece = recv_b[step, s]
+                block = jnp.where(
+                    lane_b == s, pltpu.roll(piece, shift, 1) if shift else piece, block
+                )
+            blocks.append(block)
+        both = dot3(jnp.concatenate(blocks, axis=0), strike_hi[...], strike_lo[...])
+        both = both.reshape(dip_count, 2, group, 2 * total_x)
+        real, imag = both[:, 0], both[:, 1]
+        return (
+            real[..., :total_x] + imag[..., total_x:],
+            imag[..., :total_x] - real[..., total_x:],
+        )
+
+    def by_residue(ref, *lead):
+        return jnp.stack(
+            [ref[(*lead, pl.ds(k0, group, stride=dip_count), slice(None))] for k0 in range(dip_count)]
+        )
+
+    def convolve(step, spectra):
+        sum_re = by_residue(stored, step * 2)
+        sum_im = by_residue(stored, step * 2 + 1)
+        for offset, (real, imag) in enumerate(spectra):
+            weight = by_residue(weights, offset)
+            sum_re = sum_re + weight * real
+            sum_im = sum_im + weight * imag
+        return sum_re, sum_im
+
+    def strike_inverse(step, sum_re, sum_im):
+        both = jnp.stack([sum_re, sum_im], axis=1).reshape(2 * modes, total_x)
+        both = dot3(both, strike_hi[...], strike_lo[...])
+        both = both.reshape(dip_count, 2, group, 2 * total_x)
+        real, imag = both[:, 0], both[:, 1]
+        back = jnp.stack(
+            [
+                real[..., :total_x] - imag[..., total_x:],
+                imag[..., :total_x] + real[..., total_x:],
+            ],
+            axis=1,
+        ).reshape(dip_count, 2 * group, total_x)
+        for s in range(strike_count):
+            block = jnp.zeros((2 * group, LANES), jnp.float32)
+            for k0 in range(dip_count):
+                shift = rows * (k0 - s) % LANES
+                piece = back[k0]
+                block = jnp.where(
+                    lane_b == k0, pltpu.roll(piece, shift, 1) if shift else piece, block
+                )
+            send_c[step, s] = block
+
+    def dip_inverse(step):
+        packed = recv_c[step].reshape(strike_count * 2 * group, LANES)
+        lines = packed.T[: dip_count * rows]
+        out = dot3(lines, dip_hi[...], dip_lo[...])
+        real, imag = [], []
+        for k0 in range(dip_count):
+            h_re = out[k0 * rows : (k0 + 1) * rows, :cols]
+            h_im = out[k0 * rows : (k0 + 1) * rows, cols:]
+            t_re = twiddle[my_d, 0, k0 : k0 + 1, :]
+            t_im = twiddle[my_d, 1, k0 : k0 + 1, :]
+            real.append(h_re * t_re + h_im * t_im)
+            imag.append(h_im * t_re - h_re * t_im)
+        for dy in range(dip_count):
+            phases = [phase(k0, dy) for k0 in range(dip_count)]
+            send_d[step, dy] = weighted(
+                [(c, part) for (c, _), part in zip(phases, real)]
+                + [(-s, part) for (_, s), part in zip(phases, imag)]
+            )
+
+    def store_history():
+        zero = jnp.zeros((2, modes, total_x), jnp.float32)
+        common = stored_count - STEPS + 1
+
+        def term(t, j):
+            return kern[j + t + 1].astype(jnp.float32)[None] * hist[j]
+
+        def add(j, sums):
+            return tuple(total + term(t, j) for t, total in enumerate(sums))
+
+        sums = lax.fori_loop(0, common, add, (zero,) * STEPS)
+        for t in range(STEPS):
+            total = sums[t]
+            for j in range(common, stored_count - t):
+                total = total + term(t, j)
+            stored[2 * t] = total[0]
+            stored[2 * t + 1] = total[1]
+            weights[t] = kern[t].astype(jnp.float32)
+
+    b_args = ("strike", my_s, strike_count, send_b, recv_b, b_send, b_recv)
+    c_args = ("strike", my_s, strike_count, send_c, recv_c, c_send, c_recv)
+    d_args = ("dip", my_d, dip_count, send_d, recv_d, d_send, d_recv)
+
+    barrier = pltpu.get_barrier_semaphore()
+    for k in range(1, strike_count):
+        pl.semaphore_signal(
+            barrier, inc=1, device_id={"strike": ring(my_s, k, strike_count)}, device_id_type=MESH
+        )
+    for k in range(1, dip_count):
+        pl.semaphore_signal(
+            barrier, inc=1, device_id={"dip": ring(my_d, k, dip_count)}, device_id_type=MESH
+        )
+    pack_x(0, stress_in.at[0])
+    pack_y(0, lambda z: stress_in[1, z])
+    pl.semaphore_wait(barrier, strike_count + dip_count - 2)
+
+    started = []
+    halos = start_halos(0)
+    started += halos
+    store_history()
+
+    traction = traction_in[...]
+    slip = slip_in[...]
+    functional = functional_in[...]
+    spectra = []
+    stress_ref = stress_in
+    front = min(3, depth)
+    for step in range(STEPS):
+        if step == 0:
+            wait_halos(halos)
+            fill_padded(0, stress_in.at[0])
+            for z in range(front):
+                velocity_layer(0, z, vel_in, stress_in, traction)
+        top = stress_z_layer(0, stress_in) if step == 0 else stress[2, 0]
+        trial = prestress[...] + top
+        trial = trial + functional
+        weaken = jnp.maximum(0.0, 1.0 - jnp.abs(slip) / crit_slip[...])
+        strength = normal_stress[...] * (
+            dynamic_friction + (static_friction - dynamic_friction) * weaken
+        )
+        clipped = jnp.clip(trial, -strength, strength)
+        previous = traction
+        traction = jnp.where(flags[...] == 1, clipped, trial)
+        slip = slip + time_step * ((trial - traction) / damping)
+        started += start_gather(step, slip)
+        last = step == STEPS - 1
+        if step == 0:
+            for z in range(front, depth):
+                velocity_layer(0, z, vel_in, stress_in, previous)
+            pack_x(1, vel)
+            pack_y(1, lambda z: vel[z])
+            halos = start_halos(1)
+            started += halos
+        wait_gather(step)
+        dip_forward(step)
+        started += exchange_start(step, *b_args)
+        if not last:
+            wait_halos(halos)
+            stress_layers(2 * step + 1, stress_ref)
+            stress_ref = stress
+            pack_x(2 * step + 2, stress.at[0])
+            pack_y(2 * step + 2, lambda z: stress[1, z])
+            halos = start_halos(2 * step + 2)
+            started += halos
+        exchange_wait(step, *b_args)
+        spectra = [strike_forward(step)] + spectra
+        strike_inverse(step, *convolve(step, spectra))
+        started += exchange_start(step, *c_args)
+        if not last:
+            wait_halos(halos)
+            fill_padded(2 * step + 2, stress.at[0])
+            for z in range(depth):
+                velocity_layer(2 * step + 2, z, vel, stress, traction)
+            pack_x(2 * step + 3, vel)
+            pack_y(2 * step + 3, lambda z: vel[z])
+            halos = start_halos(2 * step + 3)
+            started += halos
+        exchange_wait(step, *c_args)
+        dip_inverse(step)
+        started += exchange_start(step, *d_args)
+        if not last:
+            wait_halos(halos)
+            stress_layers(2 * step + 3, stress)
+        exchange_wait(step, *d_args)
+        functional = recv_d[step, 0]
+        for i in range(1, dip_count):
+            functional = functional + recv_d[step, i]
+    slip_out[...] = slip
+    traction_out[...] = traction
+    functional_out[...] = functional
+    for copy in started:
+        copy.wait_send()
+
+
+def fits_kernel(strike_count, dip_count, rows, cols, modes, total_x):
+    group = modes // dip_count
+    return (
+        STEPS == 2
+        and strike_count > 1
+        and dip_count > 1
+        and modes % (dip_count * SUBLANES) == 0
+        and rows % SUBLANES == 0
+        and cols % LANES == 0
+        and total_x == LANES
+        and dip_count * rows <= LANES
+        and strike_count * 2 * group <= 2 * LANES
+    )
+
+
+def body(*args):
+    velocity, history = args[0], args[11]
+    strike_count = lax.axis_size("strike")
+    dip_count = lax.axis_size("dip")
+    depth, rows, cols = velocity.shape
+    modes, total_x = history.shape[2:]
+    if not fits_kernel(strike_count, dip_count, rows, cols, modes, total_x):
+        return general_body(*args)
+    group = modes // dip_count
+    total_y = cols * dip_count
+    tables = (
+        *split_table(dip_table(strike_count, group, modes, cols, total_y)),
+        *split_table(strike_table(total_x)),
+        twiddle_table(dip_count, modes, cols, total_y),
+    )
+    turns = 2 * STEPS
+    f32 = jnp.float32
+    dma = pltpu.SemaphoreType.DMA
+    scratch = [
+        pltpu.VMEM((depth, rows + 2 * SUBLANES, cols), f32),
+        pltpu.VMEM((turns, 2, depth, 2, cols), f32),
+        pltpu.VMEM((turns, 2, rows, LANES), f32),
+        pltpu.VMEM((turns, 2, depth, 2, cols), f32),
+        pltpu.VMEM((turns, 2, rows, LANES), f32),
+        pltpu.VMEM((STEPS, rows, cols), f32),
+        pltpu.VMEM((STEPS, dip_count, rows, cols), f32),
+        pltpu.VMEM((STEPS, strike_count, 2 * group, LANES), f32),
+        pltpu.VMEM((STEPS, strike_count, 2 * group, LANES), f32),
+        pltpu.VMEM((STEPS, strike_count, 2 * group, LANES), f32),
+        pltpu.VMEM((STEPS, strike_count, 2 * group, LANES), f32),
+        pltpu.VMEM((STEPS, dip_count, rows, cols), f32),
+        pltpu.VMEM((STEPS, dip_count, rows, cols), f32),
+        pltpu.VMEM((2 * STEPS, modes, total_x), f32),
+        pltpu.VMEM((STEPS, modes, total_x), f32),
+        dma((turns, 4)),
+        dma((turns, 4)),
+        dma((STEPS, dip_count)),
+        dma((STEPS, dip_count)),
+        dma((STEPS, strike_count)),
+        dma((STEPS, strike_count)),
+        dma((STEPS, strike_count)),
+        dma((STEPS, strike_count)),
+        dma((STEPS, dip_count)),
+        dma((STEPS, dip_count)),
+    ]
+    plane = jax.ShapeDtypeStruct((rows, cols), f32)
+    vmem = pl.BlockSpec(memory_space=pltpu.VMEM)
+    return pl.pallas_call(
+        functools.partial(rupture_kernel, strike_count, dip_count),
+        out_shape=(
+            jax.ShapeDtypeStruct(velocity.shape, f32),
+            jax.ShapeDtypeStruct(args[1].shape, f32),
+            plane,
+            plane,
+            plane,
+        ),
+        in_specs=[vmem] * (len(args) + len(tables)),
+        out_specs=(vmem,) * 5,
+        scratch_shapes=scratch,
+        compiler_params=pltpu.CompilerParams(collective_id=0, has_side_effects=True),
+    )(*args, *[jnp.asarray(table) for table in tables])
+
+
 def solution(mesh):
     return jax.shard_map(
         body,

time: 231 us -> 52.9 us (0.23); the launches traced: 228 us -> 52.4 us
  starting transfers between devices: 68.1 us -> 0 us
  local copies, waits for them, and re-layouts: 56.4 us -> 7.5 us
  Pallas kernels: 0 us -> 44.3 us
  waiting for transfers between devices: 38.5 us -> 0 us
  other arithmetic: 32.7 us -> 0 us
  matrix products: 29.9 us -> 0 us
    all_to_all x12 -> x0, starting transfers between devices: 46.6 us -> none  [the longest x2 8.66 us: body(): lines = lax.all_to_all(slip, 'dip', split_axis=0, concat_axis=1, tiled=True)]
    pallas_call x0 -> x1, Pallas kernels: none -> 44.3 us  [body(): pl.pallas_call(functools.partial(rupture_kernel, strike_count, dip_count)...]
    all_to_all x12 -> x0, waiting for transfers between devices: 38.4 us -> none  [the longest x2 8.79 us: body(): lax.all_to_all(partway, 'dip', split_axis=5, concat_axis=2, tiled=True)]
    dot_general x58 -> x0, matrix products: 29.9 us -> none  [contract(): return jnp.einsum(form, left, right, precision=lax.Precision.HIGHEST)]
    ppermute x16 -> x0, starting transfers between devices: 21.5 us -> none  [the longest x8 19.8 us: padded_2(): lax.ppermute(lax.slice_in_dim(block, 0, width, axis=dim), axis, backward)]
    slice x19 -> x0, local copies, waits for them, and re-layouts: 11.9 us -> none  [the longest x6 4.24 us: padded_2(): lax.slice_in_dim(block, 0, width, axis=dim)]
    add x8 -> x0, other arithmetic: 10.3 us -> none  [the longest x2 2.98 us: body(): velocity = velocity + courant * buoyancy * divergence]
    all_to_all x8 -> x0, other arithmetic: 9.62 us -> none  [the longest x2 2.91 us: body(): lax.all_to_all(partway, 'dip', split_axis=5, concat_axis=2, tiled=True)]
  transfers between devices with their start and end apart: 28 -> 0, of which waited for: 11 -> 0; matrix products, arithmetic and copies ran while one was open for 36% -> 0% of each run, Pallas kernels for 0% -> 0%
where the time goes in v1:
time: 52.9 us; the launch traced here: 52.4 us
  Pallas kernels  44.3 us (84%)
  local copies, waits for them, and re-layouts  7.5 us (14%)
  between operations  0.65 us (1%)
    pallas_call x1, Pallas kernels, body(): pl.pallas_call(functools.partial(rupture_kernel, strike_count, dip_count)...  44.3 us
    unnamed x5, local copies, waits for them, and re-layouts  7.5 us

profile of v1, /device:TPU:0, one launch (start us, length us, event | category | flops | bytes accessed | tf_op | source)
XLA Modules:
  0.0 52.4 jit_solution(16069864606651844972)
XLA Ops:
  0.6 44.3 %shard_map.209 = (f32[12,16,256]{2,1,0:T(8,128)}, f32[3,12,16,256]{3,2,1,0:T(8,128)}, f32[16,256]{1,0:T(8,128)}, f32[16,256]{1,0:T(8,128)}, f32[16,256]{1,0:T(8,128)}) custom-call(f32[12,16,256]{2,1,0:T(8,128)} %vel_in.1, f32[3,12,16,256]{3,2,1,0:T(8,128)} %stress_in.1, f32[12,16,256]{2,1,0:T(8,128)} %shear.1, f32[12,16,256]{2,1,0:T(8,128)} %buoy.1, ...), custom_call_target="tpu_custom_call" | custom-call | tf_op jit(solution)/shard_map/pallas_call | solution.py:775
  44.9 1.6 %copy.28 = f32[12,16,256]{2,1,0:T(8,128)} copy(f32[12,16,256]{2,1,0:T(8,128)} %get-tuple-element.10) | data formatting | bytes 393216
  46.5 1.9 %copy.29 = f32[3,12,16,256]{3,2,1,0:T(8,128)} copy(f32[3,12,16,256]{3,2,1,0:T(8,128)} %get-tuple-element.11) | data formatting | bytes 1179648
  48.5 1.3 %copy.30 = f32[16,256]{1,0:T(8,128)} copy(f32[16,256]{1,0:T(8,128)} %get-tuple-element.12) | data formatting | bytes 32768
  49.8 1.3 %copy.31 = f32[16,256]{1,0:T(8,128)} copy(f32[16,256]{1,0:T(8,128)} %get-tuple-element.13) | data formatting | bytes 32768
  51.1 1.3 %copy.32 = f32[16,256]{1,0:T(8,128)} copy(f32[16,256]{1,0:T(8,128)} %get-tuple-element.14) | data formatting | bytes 32768

commit v2 on v1

--- a/solution.py
+++ b/solution.py
@@ -189,6 +189,9 @@
 LANES = 128
 SUBLANES = 8
 MESH = pl.DeviceIdType.MESH
+INPUTS = 18
+KERNEL_VMEM = 40 * 2**20
+HUGE = float(np.finfo(np.float32).max)
 
 
 def split_bf16(value):
@@ -214,8 +217,8 @@
     cos, sin = np.cos(angle), np.sin(angle)
     top = np.concatenate([cos, sin], axis=-1)
     bottom = np.concatenate([-sin, cos], axis=-1)
-    table = np.stack([top, bottom], axis=1)
-    return table.reshape(strike_count * 2 * group, 2 * cols) / np.sqrt(total_y)
+    table = np.stack([top, bottom])
+    return table.reshape(2 * strike_count * group, 2 * cols) / np.sqrt(total_y)
 
 
 def twiddle_table(dip_count, modes, cols, total_y):
@@ -242,58 +245,19 @@
     return product(left_high, high) + product(left_high, low) + product(left_low, high)
 
 
-def rupture_kernel(
-    strike_count,
-    dip_count,
-    vel_in,
-    stress_in,
-    shear,
-    buoy,
-    prestress,
-    normal_stress,
-    crit_slip,
-    slip_in,
-    traction_in,
-    functional_in,
-    flags,
-    hist,
-    kern,
-    dip_hi,
-    dip_lo,
-    strike_hi,
-    strike_lo,
-    twiddle,
-    vel,
-    stress,
-    slip_out,
-    traction_out,
-    functional_out,
-    padded,
-    edge_x,
-    edge_y,
-    halo_x,
-    halo_y,
-    slip_buf,
-    gathered,
-    send_b,
-    recv_b,
-    send_c,
-    recv_c,
-    send_d,
-    recv_d,
-    stored,
-    weights,
-    edge_sem,
-    halo_sem,
-    a_send,
-    a_recv,
-    b_send,
-    b_recv,
-    c_send,
-    c_recv,
-    d_send,
-    d_recv,
-):
+def rupture_kernel(strike_count, dip_count, *refs):
+    sources, refs = refs[:INPUTS], refs[INPUTS:]
+    results, refs = refs[:5], refs[5:]
+    loaded, refs = refs[:INPUTS], refs[INPUTS:]
+    (
+        vel_in, stress_in, shear, buoy, prestress, normal_stress, crit_slip, slip_in, traction_in,
+        functional_in, flags, hist, kern, dip_hi, dip_lo, strike_hi, strike_lo, twiddle,
+    ) = loaded
+    (
+        vel, stress, planes_out, padded, edge_x, edge_y, halo_x, halo_y, shared, gathered, send_b,
+        recv_b, send_c, recv_c, lines_out, stored, weights, load_sem, save_sem, edge_sem, halo_sem,
+        a_send, a_recv, b_send, b_recv, c_send, c_recv,
+    ) = refs
     depth, rows, cols = vel_in.shape
     modes = hist.shape[2]
     total_x = hist.shape[3]
@@ -305,19 +269,19 @@
     def ring(me, offset, count):
         return lax.rem(me + offset + count, count)
 
-    def remote(src, dst, send_sem, recv_sem, axis, target):
+    def remote(src, dst, send_sem, recv_sem, target):
         return pltpu.make_async_remote_copy(
             src_ref=src,
             dst_ref=dst,
             send_sem=send_sem,
             recv_sem=recv_sem,
-            device_id={axis: target},
+            device_id=target,
             device_id_type=MESH,
         )
 
     lane = lax.broadcasted_iota(jnp.int32, (rows, LANES), 1)
     column = lax.broadcasted_iota(jnp.int32, (rows, cols), 1)
-    lane_b = lax.broadcasted_iota(jnp.int32, (2 * group, LANES), 1) // rows
+    lane_b = lax.broadcasted_iota(jnp.int32, (group, LANES), 1) // rows
 
     def pack_x(turn, field):
         edge_x[turn, 0] = field[:, rows - 2 : rows, :]
@@ -344,8 +308,7 @@
                     halo_x.at[turn, side],
                     edge_sem.at[turn, side],
                     halo_sem.at[turn, side],
-                    "strike",
-                    ring(my_s, step, strike_count),
+                    {"strike": ring(my_s, step, strike_count)},
                 )
             )
             copies.append(
@@ -354,8 +317,7 @@
                     halo_y.at[turn, side],
                     edge_sem.at[turn, side + 2],
                     halo_sem.at[turn, side + 2],
-                    "dip",
-                    ring(my_d, step, dip_count),
+                    {"dip": ring(my_d, step, dip_count)},
                 )
             )
         return copies
@@ -430,62 +392,89 @@
             stress[1, z] = stress_ref[1, z] + modulus * diff_y(turn, z, vel[z])
             stress[2, z] = stress_z_layer(z, stress_ref)
 
-    def start_gather(step, value):
-        slip_buf[step] = value
-        gathered[step, my_d] = value
+    def start_gather(turn, value):
+        shared[turn] = value
+        gathered[turn, my_d] = value
         copies = []
         for k in range(1, dip_count):
             copy = remote(
-                slip_buf.at[step],
-                gathered.at[step, my_d],
-                a_send.at[step, k],
-                a_recv.at[step, k],
-                "dip",
-                ring(my_d, k, dip_count),
+                shared.at[turn],
+                gathered.at[turn, my_d],
+                a_send.at[turn, k],
+                a_recv.at[turn, k],
+                {"dip": ring(my_d, k, dip_count)},
             )
             copy.start()
             copies.append(copy)
         return copies
 
-    def wait_gather(step):
+    def wait_gather(turn):
         for k in range(1, dip_count):
             source = ring(my_d, -k, dip_count)
             remote(
-                slip_buf.at[step],
-                gathered.at[step, source],
-                a_send.at[step, k],
-                a_recv.at[step, k],
-                "dip",
-                source,
+                shared.at[turn],
+                gathered.at[turn, source],
+                a_send.at[turn, k],
+                a_recv.at[turn, k],
+                {"dip": source},
             ).wait_recv()
 
-    def exchange_start(step, axis, me, count, send, recv, send_sem, recv_sem):
-        recv[step, me] = send[step, me]
+    def start_b(step):
+        recv_b[step, my_s] = send_b[step, my_s]
         copies = []
-        for k in range(1, count):
-            target = ring(me, k, count)
+        for k in range(1, strike_count):
+            target = ring(my_s, k, strike_count)
             copy = remote(
-                send.at[step, target],
-                recv.at[step, me],
-                send_sem.at[step, k],
-                recv_sem.at[step, k],
-                axis,
-                target,
+                send_b.at[step, target],
+                recv_b.at[step, my_s],
+                b_send.at[step, k],
+                b_recv.at[step, k],
+                {"strike": target},
             )
             copy.start()
             copies.append(copy)
         return copies
 
-    def exchange_wait(step, axis, me, count, send, recv, send_sem, recv_sem):
-        for k in range(1, count):
-            source = ring(me, -k, count)
+    def wait_b(step):
+        for k in range(1, strike_count):
+            source = ring(my_s, -k, strike_count)
             remote(
-                send.at[step, source],
-                recv.at[step, source],
-                send_sem.at[step, k],
-                recv_sem.at[step, k],
-                axis,
-                source,
+                send_b.at[step, source],
+                recv_b.at[step, source],
+                b_send.at[step, k],
+                b_recv.at[step, k],
+                {"strike": source},
+            ).wait_recv()
+
+    offsets = [
+        (i, k) for k in reversed(range(dip_count)) for i in reversed(range(strike_count)) if i or k
+    ]
+
+    def start_c(step):
+        recv_c[step, my_d, my_s] = send_c[step, my_s]
+        copies = []
+        for i, k in offsets:
+            target_s, target_d = ring(my_s, i, strike_count), ring(my_d, k, dip_count)
+            copy = remote(
+                send_c.at[step, target_s],
+                recv_c.at[step, my_d, my_s],
+                c_send.at[step, k, i],
+                c_recv.at[step, k, i],
+                {"strike": target_s, "dip": target_d},
+            )
+            copy.start()
+            copies.append(copy)
+        return copies
+
+    def wait_c(step):
+        for i, k in reversed(offsets):
+            source_s, source_d = ring(my_s, -i, strike_count), ring(my_d, -k, dip_count)
+            remote(
+                send_c.at[step, source_s],
+                recv_c.at[step, source_d, source_s],
+                c_send.at[step, k, i],
+                c_recv.at[step, k, i],
+                {"strike": source_s, "dip": source_d},
             ).wait_recv()
 
     def phase(k0, dy):
@@ -501,8 +490,7 @@
             total = term if total is None else total + term
         return jnp.zeros((rows, cols), jnp.float32) if total is None else total
 
-    def dip_forward(step):
-        parts = [gathered[step, i] for i in range(dip_count)]
+    def dip_forward(step, parts):
         real, imag = [], []
         for k0 in range(dip_count):
             phases = [phase(k0, dy) for dy in range(dip_count)]
@@ -512,27 +500,27 @@
             t_im = twiddle[my_d, 1, k0 : k0 + 1, :]
             real.append(u_re * t_re - u_im * t_im)
             imag.append(u_re * t_im + u_im * t_re)
-        spare = LANES - dip_count * rows
-        if spare:
-            real.append(jnp.zeros((spare, cols), jnp.float32))
-            imag.append(jnp.zeros((spare, cols), jnp.float32))
         both = jnp.concatenate(
-            [jnp.concatenate(real, axis=0), jnp.concatenate(imag, axis=0)], axis=1
+            [jnp.concatenate(real * 2, axis=0), jnp.concatenate(imag * 2, axis=0)], axis=1
         )
         out = dot3_nt(dip_hi[...], dip_lo[...], both)
-        send_b[step] = out.reshape(strike_count, 2 * group, LANES)
+        out = out.reshape(2, strike_count, group, LANES)
+        for s in range(strike_count):
+            send_b[step, s] = jnp.where(lane_b < dip_count, out[0, s], out[1, s])
 
     def strike_forward(step):
         blocks = []
         for k0 in range(dip_count):
-            block = jnp.zeros((2 * group, LANES), jnp.float32)
-            for s in range(strike_count):
-                shift = rows * (s - k0) % LANES
-                piece = recv_b[step, s]
-                block = jnp.where(
-                    lane_b == s, pltpu.roll(piece, shift, 1) if shift else piece, block
-                )
-            blocks.append(block)
+            for part in range(2):
+                place = part * dip_count + k0
+                block = jnp.zeros((group, LANES), jnp.float32)
+                for s in range(strike_count):
+                    shift = rows * (s - place) % LANES
+                    piece = recv_b[step, s]
+                    block = jnp.where(
+                        lane_b == s, pltpu.roll(piece, shift, 1) if shift else piece, block
+                    )
+                blocks.append(block)
         both = dot3(jnp.concatenate(blocks, axis=0), strike_hi[...], strike_lo[...])
         both = both.reshape(dip_count, 2, group, 2 * total_x)
         real, imag = both[:, 0], both[:, 1]
@@ -560,41 +548,55 @@
         both = dot3(both, strike_hi[...], strike_lo[...])
         both = both.reshape(dip_count, 2, group, 2 * total_x)
         real, imag = both[:, 0], both[:, 1]
-        back = jnp.stack(
-            [
-                real[..., :total_x] - imag[..., total_x:],
-                imag[..., :total_x] + real[..., total_x:],
-            ],
-            axis=1,
-        ).reshape(dip_count, 2 * group, total_x)
+        back_re = real[..., :total_x] - imag[..., total_x:]
+        back_im = imag[..., :total_x] + real[..., total_x:]
         for s in range(strike_count):
-            block = jnp.zeros((2 * group, LANES), jnp.float32)
-            for k0 in range(dip_count):
-                shift = rows * (k0 - s) % LANES
-                piece = back[k0]
-                block = jnp.where(
-                    lane_b == k0, pltpu.roll(piece, shift, 1) if shift else piece, block
-                )
+            block = jnp.zeros((group, LANES), jnp.float32)
+            for part, back in enumerate((back_re, back_im)):
+                for k0 in range(dip_count):
+                    place = part * dip_count + k0
+                    shift = rows * (place - s) % LANES
+                    piece = back[k0]
+                    block = jnp.where(
+                        lane_b == place, pltpu.roll(piece, shift, 1) if shift else piece, block
+                    )
             send_c[step, s] = block
 
     def dip_inverse(step):
-        packed = recv_c[step].reshape(strike_count * 2 * group, LANES)
-        lines = packed.T[: dip_count * rows]
-        out = dot3(lines, dip_hi[...], dip_lo[...])
+        half = dip_count * rows
+        count = strike_count * group
+        real_lines, imag_lines = [], []
+        for i in range(dip_count):
+            lines = recv_c[step, i].reshape(count, LANES).T
+            real_lines.append(lines[:half])
+            imag_lines.append(lines[half:])
+        out = dot3(jnp.concatenate(real_lines, axis=0), dip_hi[:count], dip_lo[:count])
+        out = out + dot3(jnp.concatenate(imag_lines, axis=0), dip_hi[count:], dip_lo[count:])
         real, imag = [], []
         for k0 in range(dip_count):
-            h_re = out[k0 * rows : (k0 + 1) * rows, :cols]
-            h_im = out[k0 * rows : (k0 + 1) * rows, cols:]
-            t_re = twiddle[my_d, 0, k0 : k0 + 1, :]
-            t_im = twiddle[my_d, 1, k0 : k0 + 1, :]
-            real.append(h_re * t_re + h_im * t_im)
-            imag.append(h_im * t_re - h_re * t_im)
+            sum_re = sum_im = None
+            for i in range(dip_count):
+                at = i * half + k0 * rows
+                h_re = out[at : at + rows, :cols]
+                h_im = out[at : at + rows, cols:]
+                t_re = twiddle[i, 0, k0 : k0 + 1, :]
+                t_im = twiddle[i, 1, k0 : k0 + 1, :]
+                term_re = h_re * t_re + h_im * t_im
+                term_im = h_im * t_re - h_re * t_im
+                sum_re = term_re if sum_re is None else sum_re + term_re
+                sum_im = term_im if sum_im is None else sum_im + term_im
+            real.append(sum_re)
+            imag.append(sum_im)
+        result = []
         for dy in range(dip_count):
             phases = [phase(k0, dy) for k0 in range(dip_count)]
-            send_d[step, dy] = weighted(
-                [(c, part) for (c, _), part in zip(phases, real)]
-                + [(-s, part) for (_, s), part in zip(phases, imag)]
+            result.append(
+                weighted(
+                    [(c, part) for (c, _), part in zip(phases, real)]
+                    + [(-s, part) for (_, s), part in zip(phases, imag)]
+                )
             )
+        return result
 
     def store_history():
         zero = jnp.zeros((2, modes, total_x), jnp.float32)
@@ -615,9 +617,16 @@
             stored[2 * t + 1] = total[1]
             weights[t] = kern[t].astype(jnp.float32)
 
-    b_args = ("strike", my_s, strike_count, send_b, recv_b, b_send, b_recv)
-    c_args = ("strike", my_s, strike_count, send_c, recv_c, c_send, c_recv)
-    d_args = ("dip", my_d, dip_count, send_d, recv_d, d_send, d_recv)
+    def bound_of(slip):
+        weaken = jnp.maximum(0.0, 1.0 - jnp.abs(slip) / crit_slip[...])
+        strength = normal_stress[...] * (
+            dynamic_friction + (static_friction - dynamic_friction) * weaken
+        )
+        return jnp.where(flags[...] == 1, strength, HUGE)
+
+    def slide(trial, bound, slip):
+        traction = jnp.clip(trial, -bound, bound)
+        return traction, slip + time_step * ((trial - traction) / damping)
 
     barrier = pltpu.get_barrier_semaphore()
     for k in range(1, strike_count):
@@ -628,6 +637,14 @@
         pl.semaphore_signal(
             barrier, inc=1, device_id={"dip": ring(my_d, k, dip_count)}, device_id_type=MESH
         )
+    loads = [
+        pltpu.make_async_copy(sources[i], loaded[i], load_sem.at[i]) for i in range(INPUTS)
+    ]
+    loads[1].start()
+    for i in range(INPUTS):
+        if i != 1:
+            loads[i].start()
+    loads[1].wait()
     pack_x(0, stress_in.at[0])
     pack_y(0, lambda z: stress_in[1, z])
     pl.semaphore_wait(barrier, strike_count + dip_count - 2)
@@ -635,79 +652,100 @@
     started = []
     halos = start_halos(0)
     started += halos
+    for i in range(INPUTS):
+        if i != 1:
+            loads[i].wait()
+
+    ghost = traction_in[...]
+    front = min(3, depth)
+    base = prestress[...] + functional_in[...]
+    bound = bound_of(slip_in[...])
+    wait_halos(halos)
+    fill_padded(0, stress_in.at[0])
+    for z in range(front):
+        velocity_layer(0, z, vel_in, stress_in, ghost)
+    traction, slip = slide(base + stress_z_layer(0, stress_in), bound, slip_in[...])
+    started += start_gather(0, slip)
+    for z in range(front, depth):
+        velocity_layer(0, z, vel_in, stress_in, ghost)
+    pack_x(1, vel)
+    pack_y(1, lambda z: vel[z])
+    halos = start_halos(1)
+    started += halos
+    started += start_gather(1, bound_of(slip))
     store_history()
-
-    traction = traction_in[...]
-    slip = slip_in[...]
-    functional = functional_in[...]
-    spectra = []
-    stress_ref = stress_in
-    front = min(3, depth)
-    for step in range(STEPS):
-        if step == 0:
-            wait_halos(halos)
-            fill_padded(0, stress_in.at[0])
-            for z in range(front):
-                velocity_layer(0, z, vel_in, stress_in, traction)
-        top = stress_z_layer(0, stress_in) if step == 0 else stress[2, 0]
-        trial = prestress[...] + top
-        trial = trial + functional
-        weaken = jnp.maximum(0.0, 1.0 - jnp.abs(slip) / crit_slip[...])
-        strength = normal_stress[...] * (
-            dynamic_friction + (static_friction - dynamic_friction) * weaken
-        )
-        clipped = jnp.clip(trial, -strength, strength)
-        previous = traction
-        traction = jnp.where(flags[...] == 1, clipped, trial)
-        slip = slip + time_step * ((trial - traction) / damping)
-        started += start_gather(step, slip)
-        last = step == STEPS - 1
-        if step == 0:
-            for z in range(front, depth):
-                velocity_layer(0, z, vel_in, stress_in, previous)
-            pack_x(1, vel)
-            pack_y(1, lambda z: vel[z])
-            halos = start_halos(1)
-            started += halos
-        wait_gather(step)
-        dip_forward(step)
-        started += exchange_start(step, *b_args)
-        if not last:
-            wait_halos(halos)
-            stress_layers(2 * step + 1, stress_ref)
-            stress_ref = stress
-            pack_x(2 * step + 2, stress.at[0])
-            pack_y(2 * step + 2, lambda z: stress[1, z])
-            halos = start_halos(2 * step + 2)
-            started += halos
-        exchange_wait(step, *b_args)
-        spectra = [strike_forward(step)] + spectra
-        strike_inverse(step, *convolve(step, spectra))
-        started += exchange_start(step, *c_args)
-        if not last:
-            wait_halos(halos)
-            fill_padded(2 * step + 2, stress.at[0])
-            for z in range(depth):
-                velocity_layer(2 * step + 2, z, vel, stress, traction)
-            pack_x(2 * step + 3, vel)
-            pack_y(2 * step + 3, lambda z: vel[z])
-            halos = start_halos(2 * step + 3)
-            started += halos
-        exchange_wait(step, *c_args)
-        dip_inverse(step)
-        started += exchange_start(step, *d_args)
-        if not last:
-            wait_halos(halos)
-            stress_layers(2 * step + 3, stress)
-        exchange_wait(step, *d_args)
-        functional = recv_d[step, 0]
-        for i in range(1, dip_count):
-            functional = functional + recv_d[step, i]
-    slip_out[...] = slip
-    traction_out[...] = traction
-    functional_out[...] = functional
+    wait_gather(0)
+    slips = [gathered[0, i] for i in range(dip_count)]
+    dip_forward(0, slips)
+    started += start_b(0)
+    wait_halos(halos)
+    stress_layers(1, stress_in)
+    pack_x(2, stress.at[0])
+    pack_y(2, lambda z: stress[1, z])
+    halos = start_halos(2)
+    started += halos
+    wait_b(0)
+    spectra = [strike_forward(0)]
+    strike_inverse(0, *convolve(0, spectra))
+    started += start_c(0)
+
+    wait_halos(halos)
+    fill_padded(2, stress.at[0])
+    for z in range(front):
+        velocity_layer(2, z, vel, stress, traction)
+    started += start_gather(2, prestress[...] + stress_z_layer(0, stress))
+    for z in range(front, depth):
+        velocity_layer(2, z, vel, stress, traction)
+    pack_x(3, vel)
+    pack_y(3, lambda z: vel[z])
+    halos = start_halos(3)
+    started += halos
+    wait_gather(1)
+    wait_gather(2)
+    wait_c(0)
+    functionals = dip_inverse(0)
+    for i in range(dip_count):
+        traction, slip = slide(gathered[2, i] + functionals[i], gathered[1, i], gathered[0, i])
+        lines_out[0, i] = slip
+        lines_out[1, i] = traction
+    dip_forward(1, [lines_out[0, i] for i in range(dip_count)])
+    started += start_b(1)
+    wait_halos(halos)
+    stress_layers(3, stress)
+    saves = [
+        pltpu.make_async_copy(vel, results[0], save_sem.at[0]),
+        pltpu.make_async_copy(stress, results[1], save_sem.at[1]),
+    ]
+    for copy in saves:
+        copy.start()
+    wait_b(1)
+    spectra = [strike_forward(1)] + spectra
+    strike_inverse(1, *convolve(1, spectra))
+    started += start_c(1)
+    planes_out[0] = lines_out[0, my_d]
+    planes_out[1] = lines_out[1, my_d]
     for copy in started:
         copy.wait_send()
+    wait_c(1)
+    for i, value in enumerate(dip_inverse(1)):
+        lines_out[2, i] = value
+    planes_out[2] = lines_out[2, my_d]
+    ends = [
+        pltpu.make_async_copy(planes_out.at[i], results[2 + i], save_sem.at[2 + i]) for i in range(3)
+    ]
+    for copy in ends:
+        copy.start()
+    for copy in saves + ends:
+        copy.wait()
+
+
+def copy_kernel(*refs):
+    sources, results, sems = refs[:5], refs[5:10], refs[10]
+    saves = [pltpu.make_async_copy(sources[i], results[i], sems.at[i]) for i in range(5)]
+    for save in saves:
+        save.start()
+    for save in saves:
+        save.wait()
 
 
 def fits_kernel(strike_count, dip_count, rows, cols, modes, total_x):
@@ -720,8 +758,8 @@
         and rows % SUBLANES == 0
         and cols % LANES == 0
         and total_x == LANES
-        and dip_count * rows <= LANES
-        and strike_count * 2 * group <= 2 * LANES
+        and 2 * dip_count * rows == LANES
+        and strike_count * group <= LANES
     )
 
 
@@ -743,49 +781,57 @@
     turns = 2 * STEPS
     f32 = jnp.float32
     dma = pltpu.SemaphoreType.DMA
-    scratch = [
+    operands = (*args, *[jnp.asarray(table) for table in tables])
+    shapes = (velocity.shape, args[1].shape) + ((rows, cols),) * 3
+    outs = tuple(jax.ShapeDtypeStruct(shape, f32) for shape in shapes)
+    scratch = [pltpu.VMEM(operand.shape, operand.dtype) for operand in operands] + [
+        pltpu.VMEM(velocity.shape, f32),
+        pltpu.VMEM(args[1].shape, f32),
+        pltpu.VMEM((3, rows, cols), f32),
         pltpu.VMEM((depth, rows + 2 * SUBLANES, cols), f32),
         pltpu.VMEM((turns, 2, depth, 2, cols), f32),
         pltpu.VMEM((turns, 2, rows, LANES), f32),
         pltpu.VMEM((turns, 2, depth, 2, cols), f32),
         pltpu.VMEM((turns, 2, rows, LANES), f32),
-        pltpu.VMEM((STEPS, rows, cols), f32),
-        pltpu.VMEM((STEPS, dip_count, rows, cols), f32),
-        pltpu.VMEM((STEPS, strike_count, 2 * group, LANES), f32),
-        pltpu.VMEM((STEPS, strike_count, 2 * group, LANES), f32),
-        pltpu.VMEM((STEPS, strike_count, 2 * group, LANES), f32),
-        pltpu.VMEM((STEPS, strike_count, 2 * group, LANES), f32),
-        pltpu.VMEM((STEPS, dip_count, rows, cols), f32),
-        pltpu.VMEM((STEPS, dip_count, rows, cols), f32),
+        pltpu.VMEM((3, rows, cols), f32),
+        pltpu.VMEM((3, dip_count, rows, cols), f32),
+        pltpu.VMEM((STEPS, strike_count, group, LANES), f32),
+        pltpu.VMEM((STEPS, strike_count, group, LANES), f32),
+        pltpu.VMEM((STEPS, strike_count, group, LANES), f32),
+        pltpu.VMEM((STEPS, dip_count, strike_count, group, LANES), f32),
+        pltpu.VMEM((3, dip_count, rows, cols), f32),
         pltpu.VMEM((2 * STEPS, modes, total_x), f32),
         pltpu.VMEM((STEPS, modes, total_x), f32),
+        dma((len(operands),)),
+        dma((len(outs),)),
         dma((turns, 4)),
         dma((turns, 4)),
-        dma((STEPS, dip_count)),
-        dma((STEPS, dip_count)),
+        dma((3, dip_count)),
+        dma((3, dip_count)),
         dma((STEPS, strike_count)),
         dma((STEPS, strike_count)),
-        dma((STEPS, strike_count)),
-        dma((STEPS, strike_count)),
-        dma((STEPS, dip_count)),
-        dma((STEPS, dip_count)),
+        dma((STEPS, dip_count, strike_count)),
+        dma((STEPS, dip_count, strike_count)),
     ]
-    plane = jax.ShapeDtypeStruct((rows, cols), f32)
-    vmem = pl.BlockSpec(memory_space=pltpu.VMEM)
+    anywhere = pl.BlockSpec(memory_space=pl.ANY)
+    results = pl.pallas_call(
+        functools.partial(rupture_kernel, strike_count, dip_count),
+        out_shape=outs,
+        in_specs=[pl.BlockSpec(memory_space=pltpu.HBM)] * len(operands),
+        out_specs=(anywhere,) * len(outs),
+        scratch_shapes=scratch,
+        compiler_params=pltpu.CompilerParams(
+            collective_id=0, has_side_effects=True, vmem_limit_bytes=KERNEL_VMEM
+        ),
+    )(*operands)
     return pl.pallas_call(
-        functools.partial(rupture_kernel, strike_count, dip_count),
-        out_shape=(
-            jax.ShapeDtypeStruct(velocity.shape, f32),
-            jax.ShapeDtypeStruct(args[1].shape, f32),
-            plane,
-            plane,
-            plane,
-        ),
-        in_specs=[vmem] * (len(args) + len(tables)),
-        out_specs=(vmem,) * 5,
-        scratch_shapes=scratch,
-        compiler_params=pltpu.CompilerParams(collective_id=0, has_side_effects=True),
-    )(*args, *[jnp.asarray(table) for table in tables])
+        copy_kernel,
+        out_shape=outs,
+        in_specs=[anywhere] * len(outs),
+        out_specs=(anywhere,) * len(outs),
+        scratch_shapes=[dma((len(outs),))],
+        compiler_params=pltpu.CompilerParams(vmem_limit_bytes=KERNEL_VMEM),
+    )(*results)
 
 
 def solution(mesh):

time: 52.9 us -> 55.9 us (1.057)
  local copies, waits for them, and re-layouts: 7.5 us -> 15.7 us
  Pallas kernels: 44.3 us -> 38.6 us
    unnamed x5 -> x36, local copies, waits for them, and re-layouts: 7.5 us -> 15.7 us
    pallas_call x1, Pallas kernels: 44.3 us -> 37.6 us  [body(): pl.pallas_call(functools.partial(rupture_kernel, strike_count, dip_count)...]
    pallas_call x0 -> x1, Pallas kernels: none -> 0.93 us  [body(): pl.pallas_call(copy_kernel, out_shape=outs, in_specs=[anywhere] * len(out...]
where the time goes in v2:
time: 55.9 us; the launch traced here: 55 us
  Pallas kernels  38.6 us (69%)
  local copies, waits for them, and re-layouts  15.7 us (28%)
  between operations  0.67 us (1%)
    pallas_call x1, Pallas kernels, body(): pl.pallas_call(functools.partial(rupture_kernel, strike_count, dip_count)...  37.6 us
    unnamed x36, local copies, waits for them, and re-layouts  15.7 us

profile of v2, /device:TPU:0, one launch (start us, length us, event | category | flops | bytes accessed | tf_op | source)
XLA Modules:
  0.0 55.0 jit_solution(16250884977685823951)
XLA Ops:
  0.6 0.0 copy-start
  0.6 1.6 %copy-done = f32[64,2,32,128]{3,2,1,0:T(8,128)S(1)} copy-done((f32[64,2,32,128]{3,2,1,0:T(8,128)S(1)}, f32[64,2,32,128]{3,2,1,0:T(8,128)}, u32[]{:S(2)}) %copy-start) | copy-done | bytes 2097176
  2.2 0.0 copy-start.1
  2.2 1.1 %copy-done.1 = f32[3,12,16,256]{3,2,1,0:T(8,128)S(1)} copy-done((f32[3,12,16,256]{3,2,1,0:T(8,128)S(1)}, f32[3,12,16,256]{3,2,1,0:T(8,128)}, u32[]{:S(2)}) %copy-start.1) | copy-done | bytes 589848
  3.3 0.0 copy-start.2
  3.3 1.0 %copy-done.2 = bf16[65,32,128]{2,1,0:T(8,128)(2,1)S(1)} copy-done((bf16[65,32,128]{2,1,0:T(8,128)(2,1)S(1)}, bf16[65,32,128]{2,1,0:T(8,128)(2,1)}, u32[]{:S(2)}) %copy-start.2) | copy-done | bytes 532504
  4.3 0.0 copy-start.3
  4.3 0.9 %copy-done.3 = f32[12,16,256]{2,1,0:T(8,128)S(1)} copy-done((f32[12,16,256]{2,1,0:T(8,128)S(1)}, f32[12,16,256]{2,1,0:T(8,128)}, u32[]{:S(2)}) %copy-start.3) | copy-done | bytes 196632
  5.3 0.0 copy-start.4
  5.3 0.9 %copy-done.4 = f32[12,16,256]{2,1,0:T(8,128)S(1)} copy-done((f32[12,16,256]{2,1,0:T(8,128)S(1)}, f32[12,16,256]{2,1,0:T(8,128)}, u32[]{:S(2)}) %copy-start.4) | copy-done | bytes 196632
  6.2 0.0 copy-start.5
  6.2 0.9 %copy-done.5 = f32[12,16,256]{2,1,0:T(8,128)S(1)} copy-done((f32[12,16,256]{2,1,0:T(8,128)S(1)}, f32[12,16,256]{2,1,0:T(8,128)}, u32[]{:S(2)}) %copy-start.5) | copy-done | bytes 196632
  7.1 0.0 copy-start.6
  7.1 0.9 %copy-done.6 = bf16[128,512]{1,0:T(8,128)(2,1)S(1)} copy-done((bf16[128,512]{1,0:T(8,128)(2,1)S(1)}, bf16[128,512]{1,0:T(8,128)(2,1)}, u32[]{:S(2)}) %copy-start.6) | copy-done | bytes 131096
  8.0 0.0 copy-start.7
  8.0 0.9 %copy-done.7 = bf16[128,512]{1,0:T(8,128)(2,1)S(1)} copy-done((bf16[128,512]{1,0:T(8,128)(2,1)S(1)}, bf16[128,512]{1,0:T(8,128)(2,1)}, u32[]{:S(2)}) %copy-start.7) | copy-done | bytes 131096
  8.9 0.0 copy-start.8
  8.9 0.8 %copy-done.8 = bf16[128,256]{1,0:T(8,128)(2,1)S(1)} copy-done((bf16[128,256]{1,0:T(8,128)(2,1)S(1)}, bf16[128,256]{1,0:T(8,128)(2,1)}, u32[]{:S(2)}) %copy-start.8) | copy-done | bytes 65560
  9.8 0.0 copy-start.9
  9.8 0.8 %copy-done.9 = bf16[128,256]{1,0:T(8,128)(2,1)S(1)} copy-done((bf16[128,256]{1,0:T(8,128)(2,1)S(1)}, bf16[128,256]{1,0:T(8,128)(2,1)}, u32[]{:S(2)}) %copy-start.9) | copy-done | bytes 65560
  10.6 0.0 copy-start.10
  10.6 0.8 %copy-done.10 = f32[4,2,4,256]{3,2,1,0:T(4,128)S(1)} copy-done((f32[4,2,4,256]{3,2,1,0:T(4,128)S(1)}, f32[4,2,4,256]{3,2,1,0:T(4,128)}, u32[]{:S(2)}) %copy-start.10) | copy-done | bytes 32792
  11.4 0.0 copy-start.11
  11.4 0.7 %copy-done.11 = f32[16,256]{1,0:T(8,128)S(1)} copy-done((f32[16,256]{1,0:T(8,128)S(1)}, f32[16,256]{1,0:T(8,128)}, u32[]{:S(2)}) %copy-start.11) | copy-done | bytes 16408
  12.1 0.0 copy-start.12
  12.1 0.7 %copy-done.12 = f32[16,256]{1,0:T(8,128)S(1)} copy-done((f32[16,256]{1,0:T(8,128)S(1)}, f32[16,256]{1,0:T(8,128)}, u32[]{:S(2)}) %copy-start.12) | copy-done | bytes 16408
  12.8 0.0 copy-start.13
  12.8 0.7 %copy-done.13 = f32[16,256]{1,0:T(8,128)S(1)} copy-done((f32[16,256]{1,0:T(8,128)S(1)}, f32[16,256]{1,0:T(8,128)}, u32[]{:S(2)}) %copy-start.13) | copy-done | bytes 16408
  13.5 0.0 copy-start.14
  13.5 0.7 %copy-done.14 = f32[16,256]{1,0:T(8,128)S(1)} copy-done((f32[16,256]{1,0:T(8,128)S(1)}, f32[16,256]{1,0:T(8,128)}, u32[]{:S(2)}) %copy-start.14) | copy-done | bytes 16408
  14.2 0.0 copy-start.15
  14.2 0.7 %copy-done.15 = f32[16,256]{1,0:T(8,128)S(1)} copy-done((f32[16,256]{1,0:T(8,128)S(1)}, f32[16,256]{1,0:T(8,128)}, u32[]{:S(2)}) %copy-start.15) | copy-done | bytes 16408
  15.0 0.0 copy-start.16
  15.0 0.7 %copy-done.16 = f32[16,256]{1,0:T(8,128)S(1)} copy-done((f32[16,256]{1,0:T(8,128)S(1)}, f32[16,256]{1,0:T(8,128)}, u32[]{:S(2)}) %copy-start.16) | copy-done | bytes 16408
  15.7 0.0 copy-start.17
  15.7 0.7 %copy-done.17 = s32[16,256]{1,0:T(8,128)S(1)} copy-done((s32[16,256]{1,0:T(8,128)S(1)}, s32[16,256]{1,0:T(8,128)}, u32[]{:S(2)}) %copy-start.17) | copy-done | bytes 16408
  16.4 37.6 %shard_map.209 = (f32[12,16,256]{2,1,0:T(8,128)S(1)}, f32[3,12,16,256]{3,2,1,0:T(8,128)S(1)}, f32[16,256]{1,0:T(8,128)S(1)}, f32[16,256]{1,0:T(8,128)S(1)}, f32[16,256]{1,0:T(8,128)S(1)}) custom-call(f32[12,16,256]{2,1,0:T(8,128)S(1)} %copy-done.3, f32[3,12,16,256]{3,2,1,0:T(8,128)S(1)} %copy-done.1, f32[12,16,256]{2,1,0:T(8,128)S(1)} %copy-done.4, ...), custom_call_target="tpu_custom_call" | custom-call | tf_op jit(solution)/shard_map/pallas_call | solution.py:817
  54.0 0.9 %shard_map.210 = (f32[12,16,256]{2,1,0:T(8,128)}, f32[3,12,16,256]{3,2,1,0:T(8,128)}, f32[16,256]{1,0:T(8,128)}, f32[16,256]{1,0:T(8,128)}, f32[16,256]{1,0:T(8,128)}) custom-call(f32[12,16,256]{2,1,0:T(8,128)S(1)} %get-tuple-element.10.refs_0_, f32[3,12,16,256]{3,2,1,0:T(8,128)S(1)} %get-tuple-element.11.refs_1_, f32[16,256]{1,0:T(8,128)S(1)} %get-tuple-element.12.refs_2_, ...), custom_call_target="tpu_custom_call" | custom-call | tf_op jit(solution)/shard_map/pallas_call | solution.py:827
Async XLA Ops:
  0.6 1.6 %copy-start = (f32[64,2,32,128]{3,2,1,0:T(8,128)S(1)}, f32[64,2,32,128]{3,2,1,0:T(8,128)}, u32[]{:S(2)}) copy-start(f32[64,2,32,128]{3,2,1,0:T(8,128)} %refs_11_.1) | copy-start | bytes 6291460
  2.2 1.1 %copy-start.1 = (f32[3,12,16,256]{3,2,1,0:T(8,128)S(1)}, f32[3,12,16,256]{3,2,1,0:T(8,128)}, u32[]{:S(2)}) copy-start(f32[3,12,16,256]{3,2,1,0:T(8,128)} %refs_1_.1) | copy-start | bytes 1769476
  3.3 1.0 %copy-start.2 = (bf16[65,32,128]{2,1,0:T(8,128)(2,1)S(1)}, bf16[65,32,128]{2,1,0:T(8,128)(2,1)}, u32[]{:S(2)}) copy-start(bf16[65,32,128]{2,1,0:T(8,128)(2,1)} %refs_12_.1) | copy-start | bytes 1597444
  4.3 0.9 %copy-start.3 = (f32[12,16,256]{2,1,0:T(8,128)S(1)}, f32[12,16,256]{2,1,0:T(8,128)}, u32[]{:S(2)}) copy-start(f32[12,16,256]{2,1,0:T(8,128)} %refs_0_.1) | copy-start | bytes 589828
  5.3 0.9 %copy-start.4 = (f32[12,16,256]{2,1,0:T(8,128)S(1)}, f32[12,16,256]{2,1,0:T(8,128)}, u32[]{:S(2)}) copy-start(f32[12,16,256]{2,1,0:T(8,128)} %refs_2_.1) | copy-start | bytes 589828
  6.2 0.9 %copy-start.5 = (f32[12,16,256]{2,1,0:T(8,128)S(1)}, f32[12,16,256]{2,1,0:T(8,128)}, u32[]{:S(2)}) copy-start(f32[12,16,256]{2,1,0:T(8,128)} %refs_3_.1) | copy-start | bytes 589828
  7.1 0.9 %copy-start.6 = (bf16[128,512]{1,0:T(8,128)(2,1)S(1)}, bf16[128,512]{1,0:T(8,128)(2,1)}, u32[]{:S(2)}) copy-start(bf16[128,512]{1,0:T(8,128)(2,1)} %constant.11.clone.refs_14_) | copy-start | bytes 393220
  8.0 0.9 %copy-start.7 = (bf16[128,512]{1,0:T(8,128)(2,1)S(1)}, bf16[128,512]{1,0:T(8,128)(2,1)}, u32[]{:S(2)}) copy-start(bf16[128,512]{1,0:T(8,128)(2,1)} %constant.10.clone.refs_13_) | copy-start | bytes 393220
  8.9 0.8 %copy-start.8 = (bf16[128,256]{1,0:T(8,128)(2,1)S(1)}, bf16[128,256]{1,0:T(8,128)(2,1)}, u32[]{:S(2)}) copy-start(bf16[128,256]{1,0:T(8,128)(2,1)} %constant.13.clone.refs_16_) | copy-start | bytes 196612
  9.8 0.8 %copy-start.9 = (bf16[128,256]{1,0:T(8,128)(2,1)S(1)}, bf16[128,256]{1,0:T(8,128)(2,1)}, u32[]{:S(2)}) copy-start(bf16[128,256]{1,0:T(8,128)(2,1)} %constant.12.clone.refs_15_) | copy-start | bytes 196612
  10.6 0.8 %copy-start.10 = (f32[4,2,4,256]{3,2,1,0:T(4,128)S(1)}, f32[4,2,4,256]{3,2,1,0:T(4,128)}, u32[]{:S(2)}) copy-start(f32[4,2,4,256]{3,2,1,0:T(4,128)} %constant.14.clone.refs_17_) | copy-start | bytes 98308
  11.4 0.7 %copy-start.11 = (f32[16,256]{1,0:T(8,128)S(1)}, f32[16,256]{1,0:T(8,128)}, u32[]{:S(2)}) copy-start(f32[16,256]{1,0:T(8,128)} %refs_4_.1) | copy-start | bytes 49156
  12.1 0.7 %copy-start.12 = (f32[16,256]{1,0:T(8,128)S(1)}, f32[16,256]{1,0:T(8,128)}, u32[]{:S(2)}) copy-start(f32[16,256]{1,0:T(8,128)} %refs_5_.1) | copy-start | bytes 49156
  12.8 0.7 %copy-start.13 = (f32[16,256]{1,0:T(8,128)S(1)}, f32[16,256]{1,0:T(8,128)}, u32[]{:S(2)}) copy-start(f32[16,256]{1,0:T(8,128)} %refs_6_.1) | copy-start | bytes 49156
  13.5 0.7 %copy-start.14 = (f32[16,256]{1,0:T(8,128)S(1)}, f32[16,256]{1,0:T(8,128)}, u32[]{:S(2)}) copy-start(f32[16,256]{1,0:T(8,128)} %refs_7_.1) | copy-start | bytes 49156
  14.2 0.7 %copy-start.15 = (f32[16,256]{1,0:T(8,128)S(1)}, f32[16,256]{1,0:T(8,128)}, u32[]{:S(2)}) copy-start(f32[16,256]{1,0:T(8,128)} %refs_8_.1) | copy-start | bytes 49156
  15.0 0.7 %copy-start.16 = (f32[16,256]{1,0:T(8,128)S(1)}, f32[16,256]{1,0:T(8,128)}, u32[]{:S(2)}) copy-start(f32[16,256]{1,0:T(8,128)} %refs_9_.1) | copy-start | bytes 49156
  15.7 0.7 %copy-start.17 = (s32[16,256]{1,0:T(8,128)S(1)}, s32[16,256]{1,0:T(8,128)}, u32[]{:S(2)}) copy-start(s32[16,256]{1,0:T(8,128)} %refs_10_.1) | copy-start | bytes 49156

commit v3 on v2

--- a/solution.py
+++ b/solution.py
@@ -190,7 +190,7 @@
 SUBLANES = 8
 MESH = pl.DeviceIdType.MESH
 INPUTS = 18
-KERNEL_VMEM = 40 * 2**20
+KERNEL_VMEM = 67043328 - 1000000
 HUGE = float(np.finfo(np.float32).max)
 
 
@@ -784,6 +784,7 @@
     operands = (*args, *[jnp.asarray(table) for table in tables])
     shapes = (velocity.shape, args[1].shape) + ((rows, cols),) * 3
     outs = tuple(jax.ShapeDtypeStruct(shape, f32) for shape in shapes)
+    held = tuple(pltpu.VMEM(shape, f32) for shape in shapes)
     scratch = [pltpu.VMEM(operand.shape, operand.dtype) for operand in operands] + [
         pltpu.VMEM(velocity.shape, f32),
         pltpu.VMEM(args[1].shape, f32),
@@ -816,7 +817,7 @@
     anywhere = pl.BlockSpec(memory_space=pl.ANY)
     results = pl.pallas_call(
         functools.partial(rupture_kernel, strike_count, dip_count),
-        out_shape=outs,
+        out_shape=held,
         in_specs=[pl.BlockSpec(memory_space=pltpu.HBM)] * len(operands),
         out_specs=(anywhere,) * len(outs),
         scratch_shapes=scratch,
@@ -830,7 +831,7 @@
         in_specs=[anywhere] * len(outs),
         out_specs=(anywhere,) * len(outs),
         scratch_shapes=[dma((len(outs),))],
-        compiler_params=pltpu.CompilerParams(vmem_limit_bytes=KERNEL_VMEM),
+        compiler_params=pltpu.CompilerParams(vmem_limit_bytes=2**20),
     )(*results)
 
 

time: 55.9 us -> 39.4 us (0.70); the launches traced: 55 us -> 39.2 us
  local copies, waits for them, and re-layouts: 15.7 us -> 0 us
    unnamed x36 -> x0, local copies, waits for them, and re-layouts: 15.7 us -> none
where the time goes in v3:
time: 39.4 us; the launch traced here: 39.2 us
  Pallas kernels  38.6 us (98%)
  between operations  0.64 us (2%)
    pallas_call x1, Pallas kernels, body(): pl.pallas_call(functools.partial(rupture_kernel, strike_count, dip_count)...  37.7 us
    pallas_call x1, Pallas kernels, body(): pl.pallas_call(copy_kernel, out_shape=outs, in_specs=[anywhere] * len(out...  0.93 us

profile of v3, /device:TPU:0, one launch (start us, length us, event | category | flops | bytes accessed | tf_op | source)
XLA Modules:
  0.0 39.2 jit_solution(3277228354568007367)
XLA Ops:
  0.6 37.7 %shard_map.209 = (f32[12,16,256]{2,1,0:T(8,128)S(1)}, f32[3,12,16,256]{3,2,1,0:T(8,128)S(1)}, f32[16,256]{1,0:T(8,128)S(1)}, f32[16,256]{1,0:T(8,128)S(1)}, f32[16,256]{1,0:T(8,128)S(1)}) custom-call(f32[12,16,256]{2,1,0:T(8,128)} %refs_0_.1, f32[3,12,16,256]{3,2,1,0:T(8,128)} %refs_1_.1, f32[12,16,256]{2,1,0:T(8,128)} %refs_2_.1, f32[12,16,256]{2,1,0:T(8,128)} %refs_3_.1, ...), custom_call_target="tpu_custom_call" | custom-call | tf_op jit(solution)/shard_map/pallas_call | solution.py:818
  38.3 0.9 %shard_map.210 = (f32[12,16,256]{2,1,0:T(8,128)}, f32[3,12,16,256]{3,2,1,0:T(8,128)}, f32[16,256]{1,0:T(8,128)}, f32[16,256]{1,0:T(8,128)}, f32[16,256]{1,0:T(8,128)}) custom-call(f32[12,16,256]{2,1,0:T(8,128)S(1)} %get-tuple-element.10.refs_0_, f32[3,12,16,256]{3,2,1,0:T(8,128)S(1)} %get-tuple-element.11.refs_1_, f32[16,256]{1,0:T(8,128)S(1)} %get-tuple-element.12.refs_2_, ...), custom_call_target="tpu_custom_call" | custom-call | tf_op jit(solution)/shard_map/pallas_call | solution.py:828
